TPU v7x, 128 devices: a whole 4x4x4 slice. The times are simulated.
128 devices in a mesh: dom: 128 (over x, y, z, core).
Axes of the slice: x: 4, y: 4, z: 4, core: 2. Of those that a mesh axis runs over, the one named last changes fastest.
Arguments:
- state: float32 [9, 56, 49152], P(None, None, 'dom'), may hold values from -18 to 18
- class_label: int32 [49152], P('dom'), may hold values from 0 to 2, as said below
- stiffness: float32 [3, 56, 56], replicated, may hold values from -0.8 to 0.8
- star: float32 [3, 9, 9, 49152], P(None, None, None, 'dom'), may hold values from -0.84 to 0.84
- face_proj: float32 [4, 21, 56], replicated, may hold values from -0.75 to 0.75
- orient_map: float32 [3, 21, 21], replicated, may hold values from -1.25 to 1.25
- flux_local: float32 [4, 9, 9, 49152], P(None, None, None, 'dom'), may hold values from -0.12 to 0.15
- flux_neigh: float32 [4, 9, 9, 49152], P(None, None, None, 'dom'), may hold values from -0.12 to 0.12
- neighbor: int32 [4, 49152], P(None, 'dom'), may hold values from 0 to 1151, as said below
- neighbor_face: int32 [4, 49152], P(None, 'dom'), may hold values from 0 to 3
- orientation: int32 [4, 49152], P(None, 'dom'), may hold values from 0 to 2
- send_list: int32 [3072, 32], P('dom'), may hold values from -1 to 383, as said below
Outputs:
- final_state: float32 [9, 56, 49152], P(None, None, 'dom')
- energy: float32 [1], replicated
Inputs may be any that keep to these rules, and one draw needn't show every extreme that they name: `class_label`: each device's block of 384 elements holds exactly 128 elements of each class 0, 1 and 2. `send_list`: row 3 (2 * 4 d + p) + g lists the local elements of device d sent to its bordering partition p for that partition's elements of class g: distinct indices followed by -1 for unused slots, at least one slot used; every device receives one row with all 32 slots used. `neighbor`: A value under 384 is another element of the same device; a value 384 + (3 p + g) * 32 + r names slot r of the row that bordering partition p sends for class g, stands only on faces of class-g elements, always names a used slot, and every used slot is named by exactly one face.
All inputs are finite; a program needn't handle non-finite values.
Results may differ from a plain program's by a relative error of at most 0.0001.
Values sent between devices are 32-bit elements; how exact they have to be, the bound alone decides.
No kernel may reach another device: no remote copies, remote signals or barrier semaphores. Data moves between devices by JAX's collectives and lax.ppermute only.
A program may use at most 256 MiB of HBM per device.

v0:
```python
import math

import jax
import jax.numpy as jnp
from jax import lax
from jax.sharding import PartitionSpec as P

ORDER = 6
CYCLES = 1


HIGH = lax.Precision.HIGHEST


def from_behind(block, axis, distance):
    devices = range(lax.axis_size(axis))
    route = [((i - distance) % len(devices), i) for i in devices]
    return lax.ppermute(block, axis, route)


def element_mix(matrix, values):
    total = None
    for q in range(matrix.shape[1]):
        term = matrix[:, q, None, :] * values[q][None, :, :]
        total = term if total is None else total + term
    return total


def apply_star(values, stiffness, star):
    total = None
    for d in range(3):
        moved = jnp.einsum("ab,qbe->qae", stiffness[d], values, precision=HIGH)
        term = element_mix(star[d], moved)
        total = term if total is None else total + term
    return total


def predict(values, stiffness, star):
    derivs = [values]
    for k in range(ORDER - 1):
        derivs.append(apply_star(derivs[-1], stiffness, star))
    return derivs


def integrate(derivs, start):
    total = None
    for k in range(ORDER):
        weight = ((start + 1.0) ** (k + 1) - float(start) ** (k + 1)) / math.factorial(k + 1)
        term = derivs[k] * weight
        total = term if total is None else total + term
    return total


def correct(
    values,
    own,
    near,
    near_face,
    near_orient,
    stiffness,
    star,
    face_proj,
    orient_map,
    flux_local,
    flux_neigh,
):
    update = apply_star(own, stiffness, star)
    for f in range(4):
        on_face = jnp.einsum("ab,qbe->qae", face_proj[f], own, precision=HIGH)
        lifted = jnp.einsum("ba,qbe->qae", face_proj[f], on_face, precision=HIGH)
        update = update - element_mix(flux_local[f], lifted)
        chosen = None
        for j in range(4):
            projected = jnp.einsum("ab,qbe->qae", face_proj[j], near[:, :, f, :], precision=HIGH)
            term = jnp.where((near_face[f] == j)[None, None, :], projected, 0.0)
            chosen = term if chosen is None else chosen + term
        aligned = None
        for h in range(3):
            turned = jnp.einsum("ab,qbe->qae", orient_map[h], chosen, precision=HIGH)
            term = jnp.where((near_orient[f] == h)[None, None, :], turned, 0.0)
            aligned = term if aligned is None else aligned + term
        lifted_near = jnp.einsum("ba,qbe->qae", face_proj[f], aligned, precision=HIGH)
        update = update - element_mix(flux_neigh[f], lifted_near)
    return values + update


def shards(
    state,
    class_label,
    stiffness,
    star,
    face_proj,
    orient_map,
    flux_local,
    flux_neigh,
    neighbor,
    neighbor_face,
    orientation,
    send_list,
):
    quant_count = state.shape[0]
    basis_count = state.shape[1]
    elements = state.shape[2]
    per_class = elements // 3
    devices = lax.axis_size("dom")
    row_count = send_list.shape[0]
    peer_count = row_count // 3
    slot_count = send_list.shape[1]
    reach_count = peer_count // 2
    ghost_count = row_count * slot_count
    offsets = [
        p - reach_count if p < reach_count else p - reach_count + 1 for p in range(peer_count)
    ]
    class_order = jnp.argsort(class_label, stable=True)
    rank_of = jnp.argsort(class_order)
    extended_rank = jnp.concatenate([rank_of, elements + jnp.arange(ghost_count, dtype=jnp.int32)])
    near_index = jnp.take(extended_rank, neighbor[:, class_order].reshape(-1), axis=0)
    near_face = neighbor_face[:, class_order]
    near_orient = orientation[:, class_order]
    star_sorted = star[:, :, :, class_order]
    local_sorted = flux_local[:, :, :, class_order]
    neigh_sorted = flux_neigh[:, :, :, class_order]
    send_flat = send_list.reshape(-1)
    send_sorted = jnp.take(rank_of, jnp.maximum(send_flat, 0), axis=0)
    send_valid = (send_flat >= 0).astype(jnp.float32)
    sorted_state = state[:, :, class_order]
    fields = [sorted_state[:, :, c * per_class : (c + 1) * per_class] for c in range(3)]
    derivs = [None, None, None]
    owns = [None, None, None]
    nears = [None, None, None]
    energies = []
    for n in range(4 * CYCLES):
        pieces = []
        for c in range(3):
            span = 2**c
            window = slice(c * per_class, (c + 1) * per_class)
            if n % span == 0:
                derivs[c] = predict(fields[c], stiffness, star_sorted[:, :, :, window])
            pieces.append(integrate(derivs[c], n % span))
        current = jnp.concatenate(pieces, axis=2)
        outgoing = (jnp.take(current, send_sorted, axis=2) * send_valid).reshape(
            quant_count, basis_count, peer_count, 3, slot_count
        )
        outbound = jnp.transpose(
            outgoing.reshape(quant_count, basis_count, peer_count, 3 * slot_count), (2, 0, 1, 3)
        )
        outbound = outbound.reshape(peer_count, quant_count, basis_count * 3 * slot_count)
        received = []
        for p in range(peer_count):
            arrived = from_behind(outbound[peer_count - 1 - p], "dom", -offsets[p])
            received.append(arrived.reshape(quant_count, basis_count, 3 * slot_count))
        ghost_values = jnp.concatenate(received, axis=2)
        extended = jnp.concatenate([current, ghost_values], axis=2)
        gathered = jnp.take(extended, near_index, axis=2).reshape(
            quant_count, basis_count, 4, elements
        )
        for c in range(3):
            span = 2**c
            window = slice(c * per_class, (c + 1) * per_class)
            if n % span == 0:
                owns[c] = pieces[c]
                nears[c] = gathered[:, :, :, window]
            else:
                owns[c] = owns[c] + pieces[c]
                nears[c] = nears[c] + gathered[:, :, :, window]
            if (n + 1) % span == 0:
                fields[c] = correct(
                    fields[c],
                    owns[c],
                    nears[c],
                    near_face[:, window],
                    near_orient[:, window],
                    stiffness,
                    star_sorted[:, :, :, window],
                    face_proj,
                    orient_map,
                    local_sorted[:, :, :, window],
                    neigh_sorted[:, :, :, window],
                )
        if (n + 1) % 4 == 0:
            energies.append(
                jnp.sum(fields[0] * fields[0])
                + jnp.sum(fields[1] * fields[1])
                + jnp.sum(fields[2] * fields[2])
            )
    totals = lax.psum(jnp.stack(energies), "dom")
    energy = totals / (devices * elements * quant_count * basis_count)
    final_sorted = jnp.concatenate(fields, axis=2)
    final_state = jnp.take(final_sorted, rank_of, axis=2)
    return (final_state, energy)


def solution(mesh):
    in_specs = (
        P(None, None, "dom"),
        P("dom"),
        P(),
        P(None, None, None, "dom"),
        P(),
        P(),
        P(None, None, None, "dom"),
        P(None, None, None, "dom"),
        P(None, "dom"),
        P(None, "dom"),
        P(None, "dom"),
        P("dom", None),
    )
    out_specs = (P(None, None, "dom"), P())
    return jax.shard_map(shards, mesh=mesh, in_specs=in_specs, out_specs=out_specs, check_vma=False)
```

profile of v0, /device:TPU:1, one launch (start us, length us, event | category | flops | bytes accessed | tf_op | source)
XLA Modules:
  0.0 1444.2 jit_solution(17035889397841479485)
XLA Ops:
  31.8 11.5 gather_fusion.1
  43.4 14.3 fusion.702
  263.5 8.6 gather_fusion.8
  312.4 11.5 gather_fusion.2
  324.0 16.2 %fusion.700 = (f32[1,9,9,128]{2,0,1,3:T(1,128)}, f32[1,9,9,128]{2,0,1,3:T(1,128)}, f32[1,9,9,128]{2,0,1,3:T(1,128)}, f32[1,9,9,128]{2,0,1,3:T(1,128)}, f32[1,9,9...) fusion(f32[4,9,9,384]{2,0,1,3:T(4,128)} %bitcast.5721), kind=kLoop, calls=%fused_computation.3248 | loop fusion | bytes 995328 | tf_op jit(solution)/shard_map/slice | solution.py:71
  384.7 11.5 gather_fusion.3
  396.2 15.9 %fusion.701 = (f32[1,9,9,128]{2,0,1,3:T(1,128)}, f32[1,9,9,128]{2,0,1,3:T(1,128)}, f32[1,9,9,128]{2,0,1,3:T(1,128)}, f32[1,9,9,128]{2,0,1,3:T(1,128)}, f32[1,9,9...) fusion(f32[4,9,9,384]{2,0,1,3:T(4,128)} %bitcast.5720), kind=kLoop, calls=%fused_computation.3249 | loop fusion | bytes 995328 | tf_op jit(solution)/shard_map/slice | solution.py:83
  603.6 12.2 gather_fusion.11
  615.8 9.8 broadcast_select_fusion.3
  746.4 10.8 collective-permute-done.9
  782.3 8.2 copy.453
  790.5 12.2 gather_fusion.13
  802.7 9.6 broadcast_select_fusion.2
  993.9 12.6 collective-permute-start.17
  1015.6 7.7 collective-permute-done.17
  1048.4 8.2 copy.478
  1056.6 12.2 gather_fusion.15
  1068.9 9.8 broadcast_select_fusion.1
  1187.0 7.7 collective-permute-start.25
  1203.3 9.4 collective-permute-done.25
  1235.6 8.2 copy.493
  1243.8 12.2 gather_fusion.17
  1256.0 9.4 broadcast_select_fusion
  1355.9 72.7 %psum.7 = f32[1]{0:T(128)} all-reduce(f32[1]{0:T(128)} %bitcast.2021), channel_id=1, replica_groups=mesh['dom'=128] {'dom'}, use_global_device_ids=true, to_apply=%region_5.8 | all-reduce | flops 1 | bytes 8 | tf_op jit(solution)/shard_map/psum | solution.py:186
  (2061 shorter events, 1106.8 us)
Async XLA Ops:
  205.7 356.2 %collective-permute-start = (f32[9,5376]{1,0:T(8,128)}, f32[9,5376]{1,0:T(8,128)}, u32[]{:S(2)}, u32[]{:S(2)}) collective-permute-start(f32[9,5376]{1,0:T(8,128)} %squeeze.221), channel_id=1, source_target_pairs={{124,0},{125,1},{126,2},{127,3},{0,4},{1,5},{2,6},{3,7},{4,8},{5,9... | collective-permute-start | bytes 580616 | tf_op jit(solution)/shard_map/ppermute | solution.py:18
  214.0 353.3 %collective-permute-start.1 = (f32[9,5376]{1,0:T(8,128)}, f32[9,5376]{1,0:T(8,128)}, u32[]{:S(2)}, u32[]{:S(2)}) collective-permute-start(f32[9,5376]{1,0:T(8,128)} %squeeze.222), channel_id=1, source_target_pairs={{125,0},{126,1},{127,2},{0,3},{1,4},{2,5},{3,6},{4,7},{5,8},{6,9},... | collective-permute-start | bytes 580616 | tf_op jit(solution)/shard_map/ppermute | solution.py:18
  219.1 350.4 %collective-permute-start.2 = (f32[9,5376]{1,0:T(8,128)}, f32[9,5376]{1,0:T(8,128)}, u32[]{:S(2)}, u32[]{:S(2)}) collective-permute-start(f32[9,5376]{1,0:T(8,128)} %squeeze.223), channel_id=1, source_target_pairs={{126,0},{127,1},{0,2},{1,3},{2,4},{3,5},{4,6},{5,7},{6,8},{7,9},{8... | collective-permute-start | bytes 580616 | tf_op jit(solution)/shard_map/ppermute | solution.py:18
  224.6 353.8 %collective-permute-start.3 = (f32[9,5376]{1,0:T(8,128)}, f32[9,5376]{1,0:T(8,128)}, u32[]{:S(2)}, u32[]{:S(2)}) collective-permute-start(f32[9,5376]{1,0:T(8,128)} %squeeze.224), channel_id=1, source_target_pairs={{127,0},{0,1},{1,2},{2,3},{3,4},{4,5},{5,6},{6,7},{7,8},{8,9},{9,1... | collective-permute-start | bytes 580616 | tf_op jit(solution)/shard_map/ppermute | solution.py:18
  228.5 351.8 %collective-permute-start.4 = (f32[9,5376]{1,0:T(8,128)}, f32[9,5376]{1,0:T(8,128)}, u32[]{:S(2)}, u32[]{:S(2)}) collective-permute-start(f32[9,5376]{1,0:T(8,128)} %squeeze.225), channel_id=1, source_target_pairs={{1,0},{2,1},{3,2},{4,3},{5,4},{6,5},{7,6},{8,7},{9,8},{10,9},{11,1... | collective-permute-start | bytes 580616 | tf_op jit(solution)/shard_map/ppermute | solution.py:18
  561.9 20.3 %collective-permute-start.5 = (f32[9,5376]{1,0:T(8,128)}, f32[9,5376]{1,0:T(8,128)S(1)}, u32[]{:S(2)}, u32[]{:S(2)}) collective-permute-start(f32[9,5376]{1,0:T(8,128)} %squeeze.226), channel_id=1, source_target_pairs={{2,0},{3,1},{4,2},{5,3},{6,4},{7,5},{8,6},{9,7},{10,8},{11,9},{12,... | collective-permute-start | bytes 580616 | tf_op jit(solution)/shard_map/ppermute | solution.py:18
  567.3 17.9 %collective-permute-start.6 = (f32[9,5376]{1,0:T(8,128)}, f32[9,5376]{1,0:T(8,128)S(1)}, u32[]{:S(2)}, u32[]{:S(2)}) collective-permute-start(f32[9,5376]{1,0:T(8,128)} %squeeze.227), channel_id=1, source_target_pairs={{3,0},{4,1},{5,2},{6,3},{7,4},{8,5},{9,6},{10,7},{11,8},{12,9},{13... | collective-permute-start | bytes 580616 | tf_op jit(solution)/shard_map/ppermute | solution.py:18
  569.5 23.1 %collective-permute-start.7 = (f32[9,5376]{1,0:T(8,128)S(1)}, f32[9,5376]{1,0:T(8,128)S(1)}, u32[]{:S(2)}, u32[]{:S(2)}) collective-permute-start(f32[9,5376]{1,0:T(8,128)S(1)} %copy-done.113), channel_id=1, source_target_pairs={{4,0},{5,1},{6,2},{7,3},{8,4},{9,5},{10,6},{11,7},{12,8},{13,9},{1... | collective-permute-start | bytes 580616 | tf_op jit(solution)/shard_map/ppermute | solution.py:18
  735.0 22.2 %collective-permute-start.9 = (f32[9,5376]{1,0:T(8,128)}, f32[9,5376]{1,0:T(8,128)S(1)}, u32[]{:S(2)}, u32[]{:S(2)}) collective-permute-start(f32[9,5376]{1,0:T(8,128)} %squeeze.246), channel_id=1, source_target_pairs={{125,0},{126,1},{127,2},{0,3},{1,4},{2,5},{3,6},{4,7},{5,8},{6,9},... | collective-permute-start | bytes 580616 | tf_op jit(solution)/shard_map/ppermute | solution.py:18
  737.1 21.3 %collective-permute-start.10 = (f32[9,5376]{1,0:T(8,128)}, f32[9,5376]{1,0:T(8,128)S(1)}, u32[]{:S(2)}, u32[]{:S(2)}) collective-permute-start(f32[9,5376]{1,0:T(8,128)} %squeeze.247), channel_id=1, source_target_pairs={{126,0},{127,1},{0,2},{1,3},{2,4},{3,5},{4,6},{5,7},{6,8},{7,9},{8... | collective-permute-start | bytes 580616 | tf_op jit(solution)/shard_map/ppermute | solution.py:18
  737.1 31.9 %collective-permute-start.11 = (f32[9,5376]{1,0:T(8,128)}, f32[9,5376]{1,0:T(8,128)}, u32[]{:S(2)}, u32[]{:S(2)}) collective-permute-start(f32[9,5376]{1,0:T(8,128)} %squeeze.248), channel_id=1, source_target_pairs={{127,0},{0,1},{1,2},{2,3},{3,4},{4,5},{5,6},{6,7},{7,8},{8,9},{9,1... | collective-permute-start | bytes 580616 | tf_op jit(solution)/shard_map/ppermute | solution.py:18
  737.1 33.7 %collective-permute-start.12 = (f32[9,5376]{1,0:T(8,128)}, f32[9,5376]{1,0:T(8,128)}, u32[]{:S(2)}, u32[]{:S(2)}) collective-permute-start(f32[9,5376]{1,0:T(8,128)} %squeeze.249), channel_id=1, source_target_pairs={{1,0},{2,1},{3,2},{4,3},{5,4},{6,5},{7,6},{8,7},{9,8},{10,9},{11,1... | collective-permute-start | bytes 580616 | tf_op jit(solution)/shard_map/ppermute | solution.py:18
  744.5 28.2 %collective-permute-start.13 = (f32[9,5376]{1,0:T(8,128)}, f32[9,5376]{1,0:T(8,128)}, u32[]{:S(2)}, u32[]{:S(2)}) collective-permute-start(f32[9,5376]{1,0:T(8,128)} %squeeze.250), channel_id=1, source_target_pairs={{2,0},{3,1},{4,2},{5,3},{6,4},{7,5},{8,6},{9,7},{10,8},{11,9},{12,... | collective-permute-start | bytes 580616 | tf_op jit(solution)/shard_map/ppermute | solution.py:18
  758.5 17.9 %collective-permute-start.15 = (f32[9,5376]{1,0:T(8,128)}, f32[9,5376]{1,0:T(8,128)}, u32[]{:S(2)}, u32[]{:S(2)}) collective-permute-start(f32[9,5376]{1,0:T(8,128)} %squeeze.252), channel_id=1, source_target_pairs={{4,0},{5,1},{6,2},{7,3},{8,4},{9,5},{10,6},{11,7},{12,8},{13,9},{1... | collective-permute-start | bytes 580616 | tf_op jit(solution)/shard_map/ppermute | solution.py:18
  993.9 29.4 %collective-permute-start.17 = (f32[9,5376]{1,0:T(8,128)}, f32[9,5376]{1,0:T(8,128)S(1)}, u32[]{:S(2)}, u32[]{:S(2)}) collective-permute-start(f32[9,5376]{1,0:T(8,128)} %squeeze.270), channel_id=1, source_target_pairs={{125,0},{126,1},{127,2},{0,3},{1,4},{2,5},{3,6},{4,7},{5,8},{6,9},... | collective-permute-start | bytes 580616 | tf_op jit(solution)/shard_map/ppermute | solution.py:18
  1006.5 21.6 %collective-permute-start.18 = (f32[9,5376]{1,0:T(8,128)}, f32[9,5376]{1,0:T(8,128)S(1)}, u32[]{:S(2)}, u32[]{:S(2)}) collective-permute-start(f32[9,5376]{1,0:T(8,128)} %squeeze.271), channel_id=1, source_target_pairs={{126,0},{127,1},{0,2},{1,3},{2,4},{3,5},{4,6},{5,7},{6,8},{7,9},{8... | collective-permute-start | bytes 580616 | tf_op jit(solution)/shard_map/ppermute | solution.py:18
  1006.6 27.1 %collective-permute-start.19 = (f32[9,5376]{1,0:T(8,128)}, f32[9,5376]{1,0:T(8,128)}, u32[]{:S(2)}, u32[]{:S(2)}) collective-permute-start(f32[9,5376]{1,0:T(8,128)} %squeeze.272), channel_id=1, source_target_pairs={{127,0},{0,1},{1,2},{2,3},{3,4},{4,5},{5,6},{6,7},{7,8},{8,9},{9,1... | collective-permute-start | bytes 580616 | tf_op jit(solution)/shard_map/ppermute | solution.py:18
  1006.6 28.9 %collective-permute-start.20 = (f32[9,5376]{1,0:T(8,128)}, f32[9,5376]{1,0:T(8,128)}, u32[]{:S(2)}, u32[]{:S(2)}) collective-permute-start(f32[9,5376]{1,0:T(8,128)} %squeeze.273), channel_id=1, source_target_pairs={{1,0},{2,1},{3,2},{4,3},{5,4},{6,5},{7,6},{8,7},{9,8},{10,9},{11,1... | collective-permute-start | bytes 580616 | tf_op jit(solution)/shard_map/ppermute | solution.py:18
  1008.7 28.6 %collective-permute-start.21 = (f32[9,5376]{1,0:T(8,128)}, f32[9,5376]{1,0:T(8,128)}, u32[]{:S(2)}, u32[]{:S(2)}) collective-permute-start(f32[9,5376]{1,0:T(8,128)} %squeeze.274), channel_id=1, source_target_pairs={{2,0},{3,1},{4,2},{5,3},{6,4},{7,5},{8,6},{9,7},{10,8},{11,9},{12,... | collective-permute-start | bytes 580616 | tf_op jit(solution)/shard_map/ppermute | solution.py:18
  1187.0 25.7 %collective-permute-start.25 = (f32[9,5376]{1,0:T(8,128)}, f32[9,5376]{1,0:T(8,128)S(1)}, u32[]{:S(2)}, u32[]{:S(2)}) collective-permute-start(f32[9,5376]{1,0:T(8,128)} %squeeze.282), channel_id=1, source_target_pairs={{125,0},{126,1},{127,2},{0,3},{1,4},{2,5},{3,6},{4,7},{5,8},{6,9},... | collective-permute-start | bytes 580616 | tf_op jit(solution)/shard_map/ppermute | solution.py:18
  1194.7 19.3 %collective-permute-start.26 = (f32[9,5376]{1,0:T(8,128)}, f32[9,5376]{1,0:T(8,128)S(1)}, u32[]{:S(2)}, u32[]{:S(2)}) collective-permute-start(f32[9,5376]{1,0:T(8,128)} %squeeze.283), channel_id=1, source_target_pairs={{126,0},{127,1},{0,2},{1,3},{2,4},{3,5},{4,6},{5,7},{6,8},{7,9},{8... | collective-permute-start | bytes 580616 | tf_op jit(solution)/shard_map/ppermute | solution.py:18
  1194.7 25.7 %collective-permute-start.27 = (f32[9,5376]{1,0:T(8,128)}, f32[9,5376]{1,0:T(8,128)}, u32[]{:S(2)}, u32[]{:S(2)}) collective-permute-start(f32[9,5376]{1,0:T(8,128)} %squeeze.284), channel_id=1, source_target_pairs={{127,0},{0,1},{1,2},{2,3},{3,4},{4,5},{5,6},{6,7},{7,8},{8,9},{9,1... | collective-permute-start | bytes 580616 | tf_op jit(solution)/shard_map/ppermute | solution.py:18
  1195.1 27.2 %collective-permute-start.28 = (f32[9,5376]{1,0:T(8,128)}, f32[9,5376]{1,0:T(8,128)}, u32[]{:S(2)}, u32[]{:S(2)}) collective-permute-start(f32[9,5376]{1,0:T(8,128)} %squeeze.285), channel_id=1, source_target_pairs={{1,0},{2,1},{3,2},{4,3},{5,4},{6,5},{7,6},{8,7},{9,8},{10,9},{11,1... | collective-permute-start | bytes 580616 | tf_op jit(solution)/shard_map/ppermute | solution.py:18
  1199.1 24.9 %collective-permute-start.29 = (f32[9,5376]{1,0:T(8,128)}, f32[9,5376]{1,0:T(8,128)}, u32[]{:S(2)}, u32[]{:S(2)}) collective-permute-start(f32[9,5376]{1,0:T(8,128)} %squeeze.286), channel_id=1, source_target_pairs={{2,0},{3,1},{4,2},{5,3},{6,4},{7,5},{8,6},{9,7},{10,8},{11,9},{12,... | collective-permute-start | bytes 580616 | tf_op jit(solution)/shard_map/ppermute | solution.py:18
  (485 other events, 11709.3 us)
where the time goes:
time: 1470 us; the launch traced here: 1440 us
  local copies, waits for them, and re-layouts  786 us (53%)
  matrix products  239 us (16%)
  other arithmetic  209 us (14%)
  blocking collectives  72.7 us (5%)
  starting transfers between devices  66.2 us (5%)
  waiting for transfers between devices  57.1 us (4%)
  between operations  14.9 us (1%)
    unnamed x1137, local copies, waits for them, and re-layouts  222 us
    mul x179, local copies, waits for them, and re-layouts, element_mix(): term = matrix[:, q, None, :] * values[q][None, :, :]  82.7 us
    psum x1, blocking collectives, shards(): totals = lax.psum(jnp.stack(energies), 'dom')  72.7 us
    dot_general x126, matrix products, apply_star(): moved = jnp.einsum('ab,qbe->qae', stiffness[d], values, precision=HIGH)  71.5 us
    ppermute x32, starting transfers between devices, from_behind(): return lax.ppermute(block, axis, route)  66.2 us
    dot_general x112, matrix products, correct(): jnp.einsum('ab,qbe->qae', face_proj[j], near[:, :, f, :], precision=HIGH)  61.8 us
    ppermute x32, waiting for transfers between devices, from_behind(): return lax.ppermute(block, axis, route)  57.1 us
    slice x36, local copies, waits for them, and re-layouts, shards(): arrived = from_behind(outbound[peer_count - 1 - p], 'dom', -offsets[p])  54.1 us
  transfers between devices with their start and end apart: 32, of which 13 were waited for; matrix products, arithmetic and copies ran while one was open for 28% of the time, Pallas kernels for 0%

commit v1 on v0

v1 whole, which is shorter than its diff:
```python
import math

import jax
import jax.numpy as jnp
from jax import lax
from jax.experimental import pallas as pl
from jax.experimental.pallas import tpu as pltpu
from jax.sharding import PartitionSpec as P

ORDER = 6
Q = 9
B = 56
FB = 21
FP = 24
L = 128
REACH = 4
PEERS = 8
SLOTS = 32
GROUP = 8
STEPS = 4
OFFSETS = [p - REACH if p < REACH else p - REACH + 1 for p in range(PEERS)]
KROWS = 3 * B
WROWS = KROWS + 4 * FP
MSG = 7
F32 = jnp.float32
BF16 = jnp.bfloat16
I32 = jnp.int32
VMEM_LIMIT = 40 * 1024 * 1024


def shape(dims, dtype=F32):
    return jax.ShapeDtypeStruct(dims, dtype)


def call(kernel, outs, scratch, name):
    return pl.pallas_call(
        kernel,
        out_shape=outs,
        scratch_shapes=scratch,
        compiler_params=pltpu.CompilerParams(vmem_limit_bytes=VMEM_LIMIT),
        name=name,
    )


def lane_take(x, index):
    numbers = lax.GatherDimensionNumbers(
        offset_dims=(),
        collapsed_slice_dims=(1,),
        start_index_map=(1,),
        operand_batching_dims=(0,),
        start_indices_batching_dims=(0,),
    )
    return lax.gather(
        x,
        index[..., None],
        numbers,
        slice_sizes=(1, 1),
        mode=lax.GatherScatterMode.PROMISE_IN_BOUNDS,
    )


def pick(blocks, code, lane):
    out = lane_take(blocks[0], lane)
    for k in range(1, len(blocks)):
        out = jnp.where(code == k, lane_take(blocks[k], lane), out)
    return out


def rows_of(vec, rows):
    return jnp.broadcast_to(vec, (rows, L))


def split(values):
    hi = values.astype(BF16)
    lo = (values - hi.astype(F32)).astype(BF16)
    return hi, lo


def put_stack(ref, q, values, rows):
    have = values.shape[0]
    if have < rows:
        values = jnp.concatenate([values, jnp.zeros((rows - have, L), F32)], axis=0)
    hi, lo = split(values)
    cols = slice(q * L, (q + 1) * L)
    ref[0:rows, cols] = hi
    ref[rows : 2 * rows, cols] = lo
    ref[2 * rows : 3 * rows, cols] = hi


def column_tiles():
    return [(t, min(2, Q - t)) for t in range(0, Q, 2)]


def product(weights, stack_ref, store, contract=1):
    for start, count in column_tiles():
        cols = slice(start * L, (start + count) * L)
        out = lax.dot_general(
            weights,
            stack_ref[:, cols],
            (((contract,), (0,)), ((), ())),
            preferred_element_type=F32,
        )
        for j in range(count):
            store(start + j, out[:, j * L : (j + 1) * L])


def mix_groups(total, most):
    groups = []
    at = 0
    while at < total:
        size = min(most, total - at)
        groups.append((at, size))
        at += size
    return groups


def row_bcast(ref, at, q):
    return ref[at, pl.ds(q, 8, stride=0), :][None]


def star_mix(star_ref, moved_ref, put):
    for r0, rn in mix_groups(B, 32):
        acc = [None] * Q
        for d in range(3):
            for q in range(Q):
                m = moved_ref[q, d * B + r0 : d * B + r0 + rn, :].reshape(rn // 8, 8, L)
                for p in range(Q):
                    term = row_bcast(star_ref, d * Q + p, q) * m
                    acc[p] = term if acc[p] is None else acc[p] + term
        for p in range(Q):
            put(p, r0, rn, acc[p].reshape(rn, L))


def class_lanes(c):
    return slice(c * L, (c + 1) * L)


def nt_dot(a, b):
    return lax.dot_general(a, b, (((1,), (1,)), ((), ())), preferred_element_type=F32)


def index_kernel(
    dev_ref, label_ref, nbr_ref, face_ref, orient_ref, send_ref, stiff_ref, proj_ref, omap_ref,
    order_ref, rank_ref, code_ref, lane_ref, sorted_orient_ref, send_blk_ref, send_lane_ref,
    req_a_ref, req_b_ref, w_ref, ow_ref, lw_ref,
    wf_ref, owf_ref, lwf_ref,
):
    n_el = label_ref.shape[1]
    wf_ref[...] = jnp.zeros_like(wf_ref)
    owf_ref[...] = jnp.zeros_like(owf_ref)
    for d in range(3):
        k = stiff_ref[d]
        hi = k.astype(BF16).astype(F32)
        rows = slice(d * B, (d + 1) * B)
        wf_ref[rows, 0:B] = hi
        wf_ref[rows, 64 : 64 + B] = hi
        wf_ref[rows, 128 : 128 + B] = k - hi
    lwf_ref[...] = jnp.zeros_like(lwf_ref)
    for j in range(4):
        k = proj_ref[j]
        hi = k.astype(BF16).astype(F32)
        rows = slice(KROWS + j * FP, KROWS + j * FP + FB)
        wf_ref[rows, 0:B] = hi
        wf_ref[rows, 64 : 64 + B] = hi
        wf_ref[rows, 128 : 128 + B] = k - hi
        lwf_ref[j * FP : j * FP + FB, :] = hi
        lwf_ref[96 + j * FP : 96 + j * FP + FB, :] = hi
        lwf_ref[192 + j * FP : 192 + j * FP + FB, :] = k - hi
    for h in range(3):
        k = omap_ref[h]
        hi = k.astype(BF16).astype(F32)
        rows = slice(h * FP, h * FP + FB)
        owf_ref[rows, 0:FB] = hi
        owf_ref[rows, 32 : 32 + FB] = hi
        owf_ref[rows, 64 : 64 + FB] = k - hi
    w_ref[...] = wf_ref[...].astype(BF16)
    ow_ref[...] = owf_ref[...].astype(BF16)
    lw_ref[...] = lwf_ref[...].astype(BF16)
    label = label_ref[...]
    classes = lax.broadcasted_iota(I32, (8, n_el), 0)
    hot = (jnp.broadcast_to(label, (8, n_el)) == classes).astype(F32)
    row = lax.broadcasted_iota(I32, (n_el, n_el), 0)
    col = lax.broadcasted_iota(I32, (n_el, n_el), 1)
    before = (row < col).astype(F32).astype(BF16)
    prefix = jnp.dot(hot.astype(BF16), before, preferred_element_type=F32)
    base = classes.astype(F32) * float(L)
    rank = jnp.sum(hot * (prefix + base), axis=0, keepdims=True).astype(I32)
    here = (jnp.broadcast_to(rank, (n_el, n_el)) == row).astype(F32).astype(BF16)
    ids = lax.broadcasted_iota(I32, (8, n_el), 1)
    first = lax.broadcasted_iota(I32, (8, n_el), 0) == 0
    parts = jnp.where(first, ids // L, ids % L).astype(F32).astype(BF16)
    order = nt_dot(parts, here).astype(I32)
    order_ref[...] = order
    rank_ref[...] = jnp.where(first, jnp.broadcast_to(rank >> 7, (8, n_el)), jnp.broadcast_to(rank & 127, (8, n_el)))
    rank_blocks = [rows_of(rank[:, class_lanes(c)], 8) for c in range(3)]
    pad = jnp.zeros((4, n_el), I32)
    tables = [jnp.concatenate([ref[...], pad], axis=0) for ref in (nbr_ref, face_ref, orient_ref)]
    sub = lax.broadcasted_iota(I32, (8, L), 0)
    lanes = lax.broadcasted_iota(I32, (8, L), 1)
    for c in range(3):
        blk = rows_of(order[0:1, class_lanes(c)], 8)
        lane = rows_of(order[1:2, class_lanes(c)], 8)
        nbr, face, orient = [
            pick([t[:, class_lanes(b)] for b in range(3)], blk, lane) for t in tables
        ]
        ghost = nbr >= n_el
        inside = jnp.where(ghost, 0, nbr)
        place = pick(rank_blocks, inside >> 7, inside & 127)
        slot = jnp.where(ghost, nbr - n_el, 0)
        peer = ((slot >> 5) * 11) >> 5
        slot = peer * SLOTS + (slot & 31)
        code_ref[c] = jnp.where(ghost, 12 + (slot >> 7), face * 3 + (place >> 7))
        lane_ref[c] = jnp.where(ghost, slot & 127, place & 127)
        sorted_orient_ref[c] = orient
        slot = jnp.where(ghost, slot, -1)
        want = jnp.zeros((8, 2 * L), F32)
        target = lax.broadcasted_iota(I32, (2 * L, L), 0)
        for f in range(4):
            match = (jnp.broadcast_to(slot[f : f + 1], (2 * L, L)) == target).astype(F32).astype(BF16)
            value = rows_of(face[f : f + 1], 8).astype(F32).astype(BF16)
            want = want + nt_dot(value, match)
        want = want.astype(I32)
        for p in range(PEERS):
            half = want[:, class_lanes(p // 4)]
            turn = (-(p % 4) * SLOTS) % L
            moved = pltpu.roll(half, turn, axis=1) if turn else half
            wf_ref[8 * p : 8 * p + 8, 0:L] = jnp.where(
                sub == c, moved.astype(F32), wf_ref[8 * p : 8 * p + 8, 0:L]
            )
    place_in_group = dev_ref[0] % GROUP
    other_place = (place_in_group + REACH) % GROUP
    for p in range(PEERS):
        message = wf_ref[8 * p : 8 * p + 8, 0:L].astype(I32)
        to = place_in_group + OFFSETS[p]
        within = jnp.logical_and(to >= 0, to < GROUP)

        @pl.when(within)
        def _():
            req_a_ref[jnp.where(within, to, 0)] = message

        @pl.when(jnp.logical_not(within))
        def _():
            req_b_ref[jnp.where(within, 0, other_place + OFFSETS[p])] = message

    send = jnp.maximum(send_ref[...], 0)
    place = pick(rank_blocks, send >> 7, send & 127)
    send_blk_ref[...] = place >> 7
    send_lane_ref[...] = place & 127


def run_steps(count, star_ref, d_ref, w_ref, stack_ref, moved_ref):
    def body(k, carry):
        for q in range(Q):
            put_stack(stack_ref, q, d_ref[k, q], 64)

        def store(q, out):
            moved_ref[q, 0:KROWS] = out

        product(w_ref[0:KROWS, :], stack_ref, store)

        def put(p, r0, rn, value):
            d_ref[k + 1, p, r0 : r0 + rn, :] = value

        star_mix(star_ref, moved_ref, put)
        return carry

    lax.fori_loop(0, count, body, 0)


def weights_between(start, end):
    return [(float(end) ** (k + 1) - float(start) ** (k + 1)) / math.factorial(k + 1) for k in range(ORDER)]


def integrate(d_ref, q, start, end):
    total = None
    for k, weight in enumerate(weights_between(start, end)):
        term = d_ref[k, q] * weight
        total = term if total is None else total + term
    return total


def traces(d_ref, w_ref, stack_ref, start, trace_ref):
    for q in range(Q):
        put_stack(stack_ref, q, integrate(d_ref, q, start, start + 1), 64)

    def store(q, out):
        trace_ref[q] = out

    product(w_ref[KROWS:WROWS, :], stack_ref, store)


def after_steps(c, d_ref, w_ref, stack_ref, own_ref, trace_refs):
    span = 2**c
    for t in range(span):
        traces(d_ref, w_ref, stack_ref, t, trace_refs[t])
    for q in range(Q):
        own_ref[q] = integrate(d_ref, q, 0, span)


def block_transpose(four, lane):
    a, b, c, d = four
    low = (lane & 64) == 0
    a, c = jnp.where(low, a, pltpu.roll(c, 64, axis=1)), jnp.where(low, pltpu.roll(a, 64, axis=1), c)
    b, d = jnp.where(low, b, pltpu.roll(d, 64, axis=1)), jnp.where(low, pltpu.roll(b, 64, axis=1), d)
    low = (lane & 32) == 0
    a, b = jnp.where(low, a, pltpu.roll(b, 32, axis=1)), jnp.where(low, pltpu.roll(a, 96, axis=1), b)
    c, d = jnp.where(low, c, pltpu.roll(d, 32, axis=1)), jnp.where(low, pltpu.roll(c, 96, axis=1), d)
    return [a, b, c, d]


def tile_at(v, k):
    t = MSG * k + v
    return (t // 3, t % 3) if t < 3 * Q else None


def pack(dev_ref, rows, req_ref, send_blk_ref, send_lane_ref, gat_ref, msg_ref, out_a_ref, out_b_ref):
    place_in_group = dev_ref[0] % GROUP
    other_place = (place_in_group + REACH) % GROUP
    lane = lax.broadcasted_iota(I32, (8, L), 1)
    for at, (g, sources) in enumerate(rows):
        for half in range(2):
            row = 2 * g + half
            code = req_ref[row : row + 1] * 3 + send_blk_ref[row : row + 1]
            code = rows_of(code, FP)
            index = rows_of(send_lane_ref[row : row + 1], FP)

            def body(q, carry):
                blocks = [sources[k % 3][q, (k // 3) * FP : (k // 3) * FP + FP, :] for k in range(12)]
                gat_ref[q] = pick(blocks, code, index)
                return carry

            lax.fori_loop(0, Q, body, 0)
            for v in range(MSG):
                four = []
                for k in range(4):
                    t = tile_at(v, k)
                    if t is None:
                        four.append(jnp.zeros((8, L), F32))
                    else:
                        four.append(gat_ref[t[0], 8 * t[1] : 8 * t[1] + 8, :])
                for k, value in enumerate(block_transpose(four, lane)):
                    msg_ref[4 * half + k, v] = value
        for p in range(PEERS):
            to = place_in_group + OFFSETS[p]
            within = jnp.logical_and(to >= 0, to < GROUP)

            @pl.when(within)
            def _():
                out_a_ref[jnp.where(within, to, 0), at] = msg_ref[p]

            @pl.when(jnp.logical_not(within))
            def _():
                out_b_ref[jnp.where(within, 0, other_place + OFFSETS[p]), at] = msg_ref[p]


def unpack(dev_ref, at, got_a_ref, got_b_ref, ghost_ref):
    place_in_group = dev_ref[0] % GROUP
    other_place = (place_in_group + REACH) % GROUP
    lane = lax.broadcasted_iota(I32, (8, L), 1)
    for half in range(2):
        found = []
        for k in range(4):
            at_group = place_in_group + OFFSETS[4 * half + k]
            within = jnp.logical_and(at_group >= 0, at_group < GROUP)
            first = got_a_ref[jnp.where(within, at_group, 0), at]
            second = got_b_ref[jnp.where(within, 0, other_place + OFFSETS[4 * half + k]), at]
            found.append(jnp.where(within, first, second))
        for v in range(MSG):
            moved = block_transpose([found[k][v] for k in range(4)], lane)
            for k in range(4):
                t = tile_at(v, k)
                if t is not None:
                    ghost_ref[half, t[0], 8 * t[1] : 8 * t[1] + 8, :] = moved[k]


def correct(
    state_ref, own_ref, sources, ghost_ref, code_ref, lane_ref, orient_ref, c,
    star_ref, fl_ref, fn_ref, w_ref, ow_ref, lw_ref,
    stack_ref, moved_ref, chosen_ref, cstack_ref, near_ref, flux_ref, fstack_ref, new_ref,
):
    for q in range(Q):
        put_stack(stack_ref, q, own_ref[q], 64)

    def store(q, out):
        moved_ref[q] = out

    product(w_ref[...], stack_ref, store)

    def put(p, r0, rn, value):
        new_ref[p, r0 : r0 + rn, :] = state_ref[p, r0 : r0 + rn, :] + value

    star_mix(star_ref, moved_ref, put)
    for f in range(4):
        code = rows_of(code_ref[c, f : f + 1, :], FP)
        index = rows_of(lane_ref[c, f : f + 1, :], FP)

        def body(q, carry):
            blocks = [sources[k % 3][q, (k // 3) * FP : (k // 3) * FP + FP, :] for k in range(12)]
            blocks += [ghost_ref[half, q] for half in range(2)]
            chosen_ref[q] = pick(blocks, code, index)
            return carry

        lax.fori_loop(0, Q, body, 0)
        for q in range(Q):
            put_stack(cstack_ref, q, chosen_ref[q], 32)
        turn = rows_of(orient_ref[c, f : f + 1, :], FP)

        def store_near(q, out):
            value = jnp.where(turn == 1, out[FP : 2 * FP], out[0:FP])
            near_ref[q, f * FP : (f + 1) * FP] = jnp.where(turn == 2, out[2 * FP :], value)

        product(ow_ref[...], cstack_ref, store_near)

    def flux_body(f, carry):
        acc = [None] * Q
        r = pl.multiple_of(f * FP, 8)
        for q in range(Q):
            mine = moved_ref[q, pl.ds(KROWS + r, FP), :].reshape(3, 8, L)
            theirs = near_ref[q, pl.ds(r, FP), :].reshape(3, 8, L)
            for p in range(Q):
                term = row_bcast(fl_ref, f * Q + p, q) * mine
                acc[p] = term if acc[p] is None else acc[p] + term
                acc[p] = acc[p] + row_bcast(fn_ref, f * Q + p, q) * theirs
        for p in range(Q):
            flux_ref[p, pl.ds(r, FP), :] = acc[p].reshape(FP, L)
        return carry

    lax.fori_loop(0, 4, flux_body, 0)
    for p in range(Q):
        put_stack(fstack_ref, p, flux_ref[p], 96)

    def subtract(p, out):
        new_ref[p] = new_ref[p] - out

    product(lw_ref[...], fstack_ref, subtract, contract=0)


def first_kernel(
    state_ref, star_ref, fl_ref, fn_ref, order_ref, w_ref,
    s_ref, star_out, fl_out, fn_out, own0, own1, own2, t00, t10, t11, t20, t21, t22, t23,
    d_ref, stack_ref, moved_ref,
):
    picks = []
    for c in range(3):
        picks.append((order_ref[0:1, class_lanes(c)], order_ref[1:2, class_lanes(c)]))

    def sort_rows(src, rows, put):
        blocks = [src[:, class_lanes(b)] for b in range(3)]
        for c in range(3):
            put(c, pick(blocks, rows_of(picks[c][0], rows), rows_of(picks[c][1], rows)))

    def sort_state(q, carry):
        def put(c, value):
            s_ref[c, q] = value
            d_ref[c, 0, q] = value

        sort_rows(state_ref[q], B, put)
        return carry

    lax.fori_loop(0, Q, sort_state, 0)

    def sort_matrix(src, dst, at, i, p):
        def put(c, value):
            dst[c, at, 0:Q, :] = value

        sort_rows(src[i, p], Q, put)

    def sort_star(p, carry):
        for d in range(3):
            sort_matrix(star_ref, star_out, d * Q + p, d, p)
        return carry

    lax.fori_loop(0, Q, sort_star, 0)

    def sort_flux(p, carry):
        for f in range(4):
            sort_matrix(fl_ref, fl_out, f * Q + p, f, p)
            sort_matrix(fn_ref, fn_out, f * Q + p, f, p)
        return carry

    lax.fori_loop(0, Q, sort_flux, 0)

    def each(c, carry):
        run_steps(ORDER - 1, star_out.at[c], d_ref.at[c], w_ref, stack_ref, moved_ref)
        return carry

    lax.fori_loop(0, 3, each, 0)
    after_steps(0, d_ref.at[0], w_ref, stack_ref, own0, [t00])
    after_steps(1, d_ref.at[1], w_ref, stack_ref, own1, [t10, t11])
    after_steps(2, d_ref.at[2], w_ref, stack_ref, own2, [t20, t21, t22, t23])


def first_pack_kernel(
    dev_ref, req_a_ref, req_b_ref, send_blk_ref, send_lane_ref, t0, t1, t2,
    req_ref, out_a_ref, out_b_ref,
    gat_ref, msg_ref,
):
    place_in_group = dev_ref[0] % GROUP
    other_place = (place_in_group + REACH) % GROUP
    lane = lax.broadcasted_iota(I32, (1, L), 1)
    rows = [jnp.zeros((1, L), I32) for _ in range(8)]
    for p in range(PEERS):
        at_group = place_in_group + OFFSETS[p]
        within = jnp.logical_and(at_group >= 0, at_group < GROUP)
        first = req_a_ref[jnp.where(within, at_group, 0)]
        second = req_b_ref[jnp.where(within, 0, other_place + OFFSETS[p])]
        message = jnp.where(within, first, second)
        turn = (p % 4) * SLOTS
        message = pltpu.roll(message, turn, axis=1) if turn else message
        part = (lane >> 5) == (p % 4)
        for g in range(3):
            row = 2 * g + p // 4
            rows[row] = jnp.where(part, message[g : g + 1], rows[row])
    for row in range(8):
        req_ref[row : row + 1] = rows[row]
    pack(dev_ref, [(0, [t0, t1, t2])], req_ref, send_blk_ref, send_lane_ref, gat_ref, msg_ref, out_a_ref, out_b_ref)


def step_kernel(n, *refs):
    refs = list(refs)

    def take(count):
        got = refs[:count]
        del refs[:count]
        return got

    ending = [c for c in range(3) if n % 2**c == 0]
    sending = [c for c in range(3) if (n + 1) % 2**c == 0] if n < STEPS else []
    last = n == STEPS
    (dev_ref, got_a, got_b, code_ref, lane_ref, orient_ref) = take(6)
    star_ref, fl_ref, fn_ref, w_ref, ow_ref, lw_ref = take(6)
    states = dict((c, take(1)[0]) for c in ending)
    owns = dict((c, take(1)[0]) for c in ending)
    sources = dict((c, take(3)) for c in ending)
    if last:
        (rank_ref,) = take(1)
        final_ref, energy_ref = take(2)
        news = None
    else:
        kept = dict((c, take(1)[0]) for c in range(3) if c not in ending)
        before = take(3) if n % 2 == 1 else None
        half_sums = take(3) if n == 3 else None
        req_ref, send_blk_ref, send_lane_ref = take(3)
        news = dict((c, take(1)[0]) for c in ending)
        new_owns = dict((c, take(1)[0]) for c in ending)
        new_traces = dict((c, take(2**c)) for c in ending)
        sums = take(3) if n % 2 == 1 else None
        full_sums = take(3) if n == 3 else None
        out_a_ref, out_b_ref = take(2)
    ghost_ref, stack_ref, moved_ref, chosen_ref, cstack_ref, near_ref, flux_ref, fstack_ref = take(8)
    if last:
        (new_scratch,) = take(1)
        news = dict((c, new_scratch.at[c]) for c in range(3))
    else:
        d_ref, msg_ref = take(2)
    for at, c in enumerate(ending):
        unpack(dev_ref, at, got_a, got_b, ghost_ref)
        correct(
            states[c], owns[c], sources[c], ghost_ref, code_ref, lane_ref, orient_ref, c,
            star_ref.at[c], fl_ref.at[c], fn_ref.at[c], w_ref, ow_ref, lw_ref,
            stack_ref, moved_ref, chosen_ref, cstack_ref, near_ref, flux_ref, fstack_ref, news[c],
        )
    if last:
        total = jnp.zeros((8, L), F32)
        for c in range(3):
            for q in range(Q):
                v = news[c][q]
                total = total + jnp.sum((v * v).reshape(B // 8, 8, L), axis=0)
        line = jnp.sum(total, axis=0, keepdims=True)
        energy_ref[...] = jnp.broadcast_to(line[None], energy_ref.shape)
        for b in range(3):
            blk = rows_of(rank_ref[0:1, class_lanes(b)], B)
            index = rows_of(rank_ref[1:2, class_lanes(b)], B)

            def unsort(q, carry):
                final_ref[q, :, class_lanes(b)] = pick([news[c][q] for c in range(3)], blk, index)
                return carry

            lax.fori_loop(0, Q, unsort, 0)
        return
    for c in ending:
        for q in range(Q):
            d_ref[0, q] = news[c][q]
        run_steps(ORDER - 1, star_ref.at[c], d_ref, w_ref, stack_ref, moved_ref)
        after_steps(c, d_ref, w_ref, stack_ref, new_owns[c], new_traces[c])
    now = [new_traces[c][0] if c in ending else kept[c] for c in range(3)]
    if sums is not None:
        for b in range(3):
            for q in range(Q):
                value = before[b][q] + now[b][q]
                sums[b][q] = value
                if full_sums is not None:
                    full_sums[b][q] = value + half_sums[b][q]
    given = {0: now, 1: sums, 2: full_sums}
    pack(
        dev_ref, [(g, given[g]) for g in sending], req_ref, send_blk_ref, send_lane_ref,
        chosen_ref, msg_ref, out_a_ref, out_b_ref,
    )


FIELD = (Q, B, L)
TRACE = (Q, 4 * FP, L)


def shards(
    state, class_label, stiffness, star, face_proj, orient_map, flux_local, flux_neigh,
    neighbor, neighbor_face, orientation, send_list,
):
    elements = state.shape[2]
    devices = lax.axis_size("dom")
    aligned = [[GROUP * k + i for i in range(GROUP)] for k in range(devices // GROUP)]
    shifted = [[(m + REACH) % devices for m in group] for group in aligned]

    def exchange(first, second):
        got_a = lax.all_to_all(first, "dom", 0, 0, axis_index_groups=aligned, tiled=True)
        got_b = lax.all_to_all(second, "dom", 0, 0, axis_index_groups=shifted, tiled=True)
        return got_a, got_b

    dev = lax.axis_index("dom").astype(I32).reshape(1)
    send = send_list.reshape(2, 4, 3, SLOTS).transpose(2, 0, 1, 3).reshape(6, L)
    send = jnp.concatenate([send, send[:2]], axis=0)
    smem = pl.BlockSpec(memory_space=pltpu.SMEM)
    whole = pl.BlockSpec(memory_space=pltpu.VMEM)

    def run(kernel, args, outs, scratch, name, with_dev=True):
        return pl.pallas_call(
            kernel,
            in_specs=[smem if with_dev and i == 0 else whole for i in range(len(args))],
            out_specs=[whole] * len(outs),
            out_shape=outs,
            scratch_shapes=scratch,
            compiler_params=pltpu.CompilerParams(vmem_limit_bytes=VMEM_LIMIT),
            name=name,
        )(*args)

    (order, rank, code, lane, orient, send_blk, send_lane, req_a, req_b, w, ow, lw) = run(
        index_kernel,
        [dev, class_label.reshape(1, elements), neighbor, neighbor_face, orientation, send, stiffness, face_proj, orient_map],
        [shape((8, elements), I32)] * 2 + [shape((3, 8, L), I32)] * 3 + [shape((8, L), I32)] * 2
        + [shape((GROUP, 8, L), I32)] * 2
        + [shape((WROWS, 192), BF16), shape((3 * FP, 96), BF16), shape((288, B), BF16)],
        [pltpu.VMEM((WROWS, 192), F32), pltpu.VMEM((3 * FP, 96), F32), pltpu.VMEM((288, B), F32)],
        "index",
    )
    got_req = exchange(req_a, req_b)
    stack = pltpu.VMEM((192, Q * L), BF16)
    moved = pltpu.VMEM((Q, WROWS, L), F32)
    (sorted_state, star_s, fl_s, fn_s, own0, own1, own2, t00, t10, t11, t20, t21, t22, t23) = run(
        first_kernel,
        [state, star, flux_local, flux_neigh, order, w],
        [shape((3,) + FIELD), shape((3, 27, 16, L)), shape((3, 36, 16, L)), shape((3, 36, 16, L))]
        + [shape(FIELD)] * 3 + [shape(TRACE)] * 7,
        [pltpu.VMEM((3, ORDER) + FIELD, F32), stack, moved],
        "first",
        with_dev=False,
    )
    gat = pltpu.VMEM((Q, FP, L), F32)
    msg = pltpu.VMEM((PEERS, MSG, 8, L), F32)
    req, out_a, out_b = run(
        first_pack_kernel,
        [dev, *got_req, send_blk, send_lane, t00, t10, t20],
        [shape((8, L), I32)] + [shape((GROUP, 1, MSG, 8, L))] * 2,
        [gat, msg],
        "first_pack",
    )
    fields = [sorted_state[c] for c in range(3)]
    owns = [own0, own1, own2]
    later = {1: {0: t10, 1: t11}, 2: {0: t20, 1: t21, 2: t22, 3: t23}}
    now = [t00, t10, t20]
    sources = {0: now}
    half_sums = None
    for n in range(1, STEPS + 1):
        ending = [c for c in range(3) if n % 2**c == 0]
        got_a, got_b = exchange(out_a, out_b)
        args = [dev, got_a, got_b, code, lane, orient, star_s, fl_s, fn_s, w, ow, lw]
        args += [fields[c] for c in ending] + [owns[c] for c in ending]
        for c in ending:
            args += sources[c]
        common = [
            pltpu.VMEM((2, Q, FP, L), F32), stack, moved, gat, pltpu.VMEM((96, Q * L), BF16),
            pltpu.VMEM(TRACE, F32), pltpu.VMEM(TRACE, F32), pltpu.VMEM((288, Q * L), BF16),
        ]

        def kernel(*refs, n=n):
            step_kernel(n, *refs)

        if n == STEPS:
            final_state, energy_out = run(
                kernel,
                args + [rank],
                [shape((Q, B, elements)), shape((devices, 1, L))],
                common + [pltpu.VMEM((3,) + FIELD, F32)],
                "last",
            )
            break
        sending = [c for c in range(3) if (n + 1) % 2**c == 0]
        kept = [c for c in range(3) if c not in ending]
        args += [later[c][n % 2**c] for c in kept]
        if n % 2 == 1:
            args += now
        if n == 3:
            args += half_sums
        args += [req, send_blk, send_lane]
        outs = [shape(FIELD)] * (2 * len(ending)) + [shape(TRACE)] * sum(2**c for c in ending)
        outs += [shape(TRACE)] * (3 if n % 2 == 1 else 0) + [shape(TRACE)] * (3 if n == 3 else 0)
        outs += [shape((GROUP, len(sending), MSG, 8, L))] * 2
        got = list(run(kernel, args, outs, common + [pltpu.VMEM((ORDER,) + FIELD, F32), msg], "step%d" % n))
        for c in ending:
            fields[c] = got.pop(0)
        for c in ending:
            owns[c] = got.pop(0)
        for c in ending:
            made = [got.pop(0) for _ in range(2**c)]
            later[c] = dict(enumerate(made))
        now = [later[c][n % 2**c] for c in range(3)]
        sources = {0: now}
        if n % 2 == 1:
            sums = [got.pop(0) for _ in range(3)]
            sources[1] = sums
            if n == 1:
                half_sums = sums
        if n == 3:
            sources[2] = [got.pop(0) for _ in range(3)]
        out_a, out_b = got
    spread = lax.all_to_all(energy_out, "dom", 0, 0, tiled=True)
    energy = jnp.sum(spread).reshape(1) / (devices * elements * Q * B)
    return final_state, energy


def solution(mesh):
    in_specs = (
        P(None, None, "dom"),
        P("dom"),
        P(),
        P(None, None, None, "dom"),
        P(),
        P(),
        P(None, None, None, "dom"),
        P(None, None, None, "dom"),
        P(None, "dom"),
        P(None, "dom"),
        P(None, "dom"),
        P("dom", None),
    )
    out_specs = (P(None, None, "dom"), P())
    return jax.shard_map(shards, mesh=mesh, in_specs=in_specs, out_specs=out_specs, check_vma=False)
```

time: 1470 us -> 283 us (0.19); the launches traced: 1440 us -> 281 us
  local copies, waits for them, and re-layouts: 786 us -> 25.2 us
  matrix products: 239 us -> 0 us
  other arithmetic: 209 us -> 0.74 us
  Pallas kernels: 0 us -> 107 us
  waiting for transfers between devices: 57.1 us -> 1.81 us
  blocking collectives: 72.7 us -> 124 us
  starting transfers between devices: 66.2 us -> 19.6 us
    dot_general x406 -> x0, matrix products: 239 us -> none  [the longest x126 71.5 us: apply_star(): moved = jnp.einsum('ab,qbe->qae', stiffness[d], values, precision=HIGH)]
    unnamed x1137 -> x102, local copies, waits for them, and re-layouts: 222 us -> 22.1 us
    slice x114 -> x2, local copies, waits for them, and re-layouts: 196 us -> 0.1 us  [shards(): send = jnp.concatenate([send, send[:2]], axis=0)]
    gather x20 -> x0, local copies, waits for them, and re-layouts: 138 us -> none  [the longest x4 48.9 us: shards(): jnp.take(extended, near_index, axis=2)]
    all_to_all x0 -> x9, blocking collectives: none -> 124 us  [the longest x5 57.1 us: exchange(): lax.all_to_all(first, 'dom', 0, 0, axis_index_groups=aligned, tiled=True)]
    pallas_call x0 -> x7, Pallas kernels: none -> 107 us  [run(): pl.pallas_call(kernel, in_specs=[smem if with_dev and i == 0 else whole f...]
    add x43 -> x0, other arithmetic: 100 us -> none  [the longest x28 35.6 us: apply_star(): total = term if total is None else total + term]
    mul x179 -> x0, local copies, waits for them, and re-layouts: 82.7 us -> none  [element_mix(): term = matrix[:, q, None, :] * values[q][None, :, :]]
  transfers between devices with their start and end apart: 32 -> 2, of which waited for: 13 -> 1; matrix products, arithmetic and copies ran while one was open for 28% -> 1% of each run, Pallas kernels for 0% -> 7%
where the time goes in v1:
time: 283 us; the launch traced here: 281 us
  blocking collectives  124 us (44%)
  Pallas kernels  107 us (38%)
  local copies, waits for them, and re-layouts  25.2 us (9%)
  starting transfers between devices  19.6 us (7%)
    pallas_call x7, Pallas kernels, run(): pl.pallas_call(kernel, in_specs=[smem if with_dev and i == 0 else whole f...  107 us
    all_to_all x5, blocking collectives, exchange(): lax.all_to_all(first, 'dom', 0, 0, axis_index_groups=aligned, tiled=True)  57.1 us
    all_to_all x3, blocking collectives, exchange(): lax.all_to_all(second, 'dom', 0, 0, axis_index_groups=shifted, tiled=True)  49.4 us
    unnamed x102, local copies, waits for them, and re-layouts  22.1 us
    all_to_all x2, starting transfers between devices, exchange(): lax.all_to_all(second, 'dom', 0, 0, axis_index_groups=shifted, tiled=True)  19.6 us
    all_to_all x1, blocking collectives, shards(): spread = lax.all_to_all(energy_out, 'dom', 0, 0, tiled=True)  18 us
  transfers between devices with their start and end apart: 2, of which 1 were waited for; matrix products, arithmetic and copies ran while one was open for 1% of the time, Pallas kernels for 7%

profile of v1, /device:TPU:1, one launch (start us, length us, event | category | flops | bytes accessed | tf_op | source)
XLA Modules:
  0.0 281.4 jit_solution(9069380678486854257)
XLA Ops:
  2.4 1.6 index.1
  4.0 11.4 %all_to_all.55.req_a_ref = s32[8,8,128]{2,1,0:T(8,128)} all-to-all(s32[8,8,128]{2,1,0:T(8,128)S(1)} %get-tuple-element.61), channel_id=1, replica_groups={{0,1,2,3,4,5,6,7},{8,9,10,11,12,13,14,15},{16,17,18,19,20,21,22,23},{24..., dimensions={0} | all-to-all | bytes 65536 | tf_op jit(solution)/shard_map/all_to_all | solution.py:615
  15.5 10.0 %all-to-all-start.1 = ((s32[8,8,128]{2,1,0:T(8,128)}), s32[8,8,128]{2,1,0:T(8,128)}, u32[]{:S(2)}, u32[]{:S(2)}) async-start(s32[8,8,128]{2,1,0:T(8,128)} %get-tuple-element.62), calls=%async_computation.1 | async-start | bytes 65536 | tf_op jit(solution)/shard_map/all_to_all | solution.py:616
  25.5 1.1 copy.21.star_ref
  27.8 1.0 copy-done.17
  28.8 18.9 %first.1 = (f32[3,9,56,128]{3,2,1,0:T(8,128)S(1)}, f32[3,27,16,128]{3,2,1,0:T(8,128)S(1)}, f32[3,36,16,128]{3,2,1,0:T(8,128)S(1)}, f32[3,36,16,128]{3,2,1,0:T(8,...) custom-call(f32[9,56,384]{2,1,0:T(8,128)S(1)} %copy-done.17, ...), custom_call_target="tpu_custom_call" | custom-call | tf_op jit(solution)/shard_map/first/pallas_call | solution.py:626
  54.6 1.0 copy-done.1
  56.3 3.2 %first_pack.1 = (s32[8,128]{1,0:T(8,128)S(1)}, f32[8,1,7,8,128]{4,3,2,1,0:T(8,128)S(1)}, f32[8,1,7,8,128]{4,3,2,1,0:T(8,128)S(1)}) custom-call(s32[1]{0:T(128)} %bitcast.dev_ref.refs_0_, s32[8,8,128]{2,1,0:T(8,128)S(1)} %copy-done.32, s32[8,8,128]{2,1,0:T(8,128)} %all-to-all-done.1.req_b_ref, ...), custom_call_target="tpu_custom_call" | custom-call | tf_op jit(solution)/shard_map/first_pack/pallas_call | solution.py:626
  59.5 9.6 %all_to_all.56.refs_1_ = f32[8,1,7,8,128]{4,3,2,1,0:T(8,128)} all-to-all(f32[8,1,7,8,128]{4,3,2,1,0:T(8,128)S(1)} %get-tuple-element.70), channel_id=1, replica_groups={{0,1,2,3,4,5,6,7},{8,9,10,11,12,13,14,15},{16,17,18,19,20,21,22,23},{24..., dimensions={0} | all-to-all | bytes 458752 | tf_op jit(solution)/shard_map/all_to_all | solution.py:615
  69.2 9.7 %all-to-all-start.3 = ((f32[8,1,7,8,128]{4,3,2,1,0:T(8,128)}), f32[8,1,7,8,128]{4,3,2,1,0:T(8,128)}, u32[]{:S(2)}, u32[]{:S(2)}) async-start(f32[8,1,7,8,128]{4,3,2,1,0:T(8,128)} %copy-done.24), calls=%async_computation.3 | async-start | bytes 458752 | tf_op jit(solution)/shard_map/all_to_all | solution.py:616
  78.8 2.1 slice_bitcast_fusion
  80.9 1.8 all-to-all-done.3.refs_2_
  85.5 1.0 copy-done.8
  90.7 16.8 %step1.1 = (f32[9,56,128]{2,1,0:T(8,128)S(1)}, f32[9,56,128]{2,1,0:T(8,128)S(1)}, f32[9,96,128]{2,1,0:T(8,128)S(1)}, f32[9,96,128]{2,1,0:T(8,128)S(1)}, f32[9,96...) custom-call(s32[1]{0:T(128)} %bitcast.dev_ref.refs_0_, ...), custom_call_target="tpu_custom_call" | custom-call | tf_op jit(solution)/shard_map/step1/pallas_call | solution.py:626
  107.6 12.1 %all_to_all.57.refs_1_ = f32[8,2,7,8,128]{4,3,2,1,0:T(8,128)S(1)} all-to-all(f32[8,2,7,8,128]{4,3,2,1,0:T(8,128)S(1)} %get-tuple-element.85), channel_id=1, replica_groups={{0,1,2,3,4,5,6,7},{8,9,10,11,12,13,14,15},{16,17,18,19,20,21,22,23},{24..., dimensions={0} | all-to-all | bytes 917504 | tf_op jit(solution)/shard_map/all_to_all | solution.py:615
  119.6 16.5 %all_to_all.58.refs_2_ = f32[8,2,7,8,128]{4,3,2,1,0:T(8,128)S(1)} all-to-all(f32[8,2,7,8,128]{4,3,2,1,0:T(8,128)S(1)} %get-tuple-element.86), channel_id=1, replica_groups={{4,5,6,7,8,9,10,11},{12,13,14,15,16,17,18,19},{20,21,22,23,24,25,26,27}..., dimensions={0} | all-to-all | bytes 917504 | tf_op jit(solution)/shard_map/all_to_all | solution.py:616
  136.8 24.6 %step2.1 = (f32[9,56,128]{2,1,0:T(8,128)S(1)}, f32[9,56,128]{2,1,0:T(8,128)S(1)}, f32[9,56,128]{2,1,0:T(8,128)S(1)}, f32[9,56,128]{2,1,0:T(8,128)S(1)}, f32[9,96...) custom-call(s32[1]{0:T(128)} %bitcast.dev_ref.refs_0_, ...), custom_call_target="tpu_custom_call" | custom-call | tf_op jit(solution)/shard_map/step2/pallas_call | solution.py:626
  161.4 9.5 %all_to_all.59.refs_1_ = f32[8,1,7,8,128]{4,3,2,1,0:T(8,128)S(1)} all-to-all(f32[8,1,7,8,128]{4,3,2,1,0:T(8,128)S(1)} %get-tuple-element.95), channel_id=1, replica_groups={{0,1,2,3,4,5,6,7},{8,9,10,11,12,13,14,15},{16,17,18,19,20,21,22,23},{24..., dimensions={0} | all-to-all | bytes 458752 | tf_op jit(solution)/shard_map/all_to_all | solution.py:615
  171.0 14.0 %all_to_all.60.refs_2_ = f32[8,1,7,8,128]{4,3,2,1,0:T(8,128)S(1)} all-to-all(f32[8,1,7,8,128]{4,3,2,1,0:T(8,128)S(1)} %get-tuple-element.96), channel_id=1, replica_groups={{4,5,6,7,8,9,10,11},{12,13,14,15,16,17,18,19},{20,21,22,23,24,25,26,27}..., dimensions={0} | all-to-all | bytes 458752 | tf_op jit(solution)/shard_map/all_to_all | solution.py:616
  184.9 18.3 %step3.1 = (f32[9,56,128]{2,1,0:T(8,128)S(1)}, f32[9,56,128]{2,1,0:T(8,128)S(1)}, f32[9,96,128]{2,1,0:T(8,128)S(1)}, f32[9,96,128]{2,1,0:T(8,128)S(1)}, f32[9,96...) custom-call(s32[1]{0:T(128)} %bitcast.dev_ref.refs_0_, ...), custom_call_target="tpu_custom_call" | custom-call | tf_op jit(solution)/shard_map/step3/pallas_call | solution.py:626
  203.3 14.4 %all_to_all.61.refs_1_ = f32[8,3,7,8,128]{4,3,2,1,0:T(8,128)S(1)} all-to-all(f32[8,3,7,8,128]{4,3,2,1,0:T(8,128)S(1)} %get-tuple-element.103), channel_id=1, replica_groups={{0,1,2,3,4,5,6,7},{8,9,10,11,12,13,14,15},{16,17,18,19,20,21,22,23},{24..., dimensions={0} | all-to-all | bytes 1376256 | tf_op jit(solution)/shard_map/all_to_all | solution.py:615
  217.7 18.9 %all_to_all.62.refs_2_ = f32[8,3,7,8,128]{4,3,2,1,0:T(8,128)S(1)} all-to-all(f32[8,3,7,8,128]{4,3,2,1,0:T(8,128)S(1)} %get-tuple-element.104), channel_id=1, replica_groups={{4,5,6,7,8,9,10,11},{12,13,14,15,16,17,18,19},{20,21,22,23,24,25,26,27}..., dimensions={0} | all-to-all | bytes 1376256 | tf_op jit(solution)/shard_map/all_to_all | solution.py:616
  237.4 23.5 %last.1 = (f32[9,56,384]{2,1,0:T(8,128)}, f32[128,1,128]{2,1,0:T(1,128)S(1)}) custom-call(s32[1]{0:T(128)} %bitcast.dev_ref.refs_0_, f32[8,3,7,8,128]{4,3,2,1,0:T(8,128)S(1)} %all_to_all.61.refs_1_, f32[8,3,7,8,128]{4,3,2,1,0:T(8,128)S(1)} %all_to_all.62.refs_2_, s32[3,8,128]{2,1,0:T(8,128)S(1)} %copy-done.26, s32[3,8,128]{2,1,0:T(8,128)S(1)} %copy-done.28, ...), custom_call_target="tpu_custom_call" | custom-call | tf_op jit(solution)/shard_map/last/pallas_call | solution.py:626
  260.9 18.0 %all_to_all.63 = f32[128,1,128]{2,1,0:T(1,128)S(1)} all-to-all(f32[128,1,128]{2,1,0:T(1,128)S(1)} %get-tuple-element.119), channel_id=1, replica_groups=mesh['dom'=128] {'dom'}, dimensions={0} | all-to-all | bytes 131072 | tf_op jit(solution)/shard_map/all_to_all | solution.py:725
  (107 shorter events, 19.6 us)
Async XLA Ops:
  4.0 11.5 %copy-start.25 = (s32[3,8,128]{2,1,0:T(8,128)}, s32[3,8,128]{2,1,0:T(8,128)S(1)}, u32[]{:S(2)}) copy-start(s32[3,8,128]{2,1,0:T(8,128)S(1)} %get-tuple-element.72.refs_3_) | copy-start | bytes 36868
  4.0 11.5 %copy-start.27 = (s32[3,8,128]{2,1,0:T(8,128)}, s32[3,8,128]{2,1,0:T(8,128)S(1)}, u32[]{:S(2)}) copy-start(s32[3,8,128]{2,1,0:T(8,128)S(1)} %get-tuple-element.73.refs_4_) | copy-start | bytes 36868
  4.0 11.5 %copy-start.29 = (s32[3,8,128]{2,1,0:T(8,128)}, s32[3,8,128]{2,1,0:T(8,128)S(1)}, u32[]{:S(2)}) copy-start(s32[3,8,128]{2,1,0:T(8,128)S(1)} %get-tuple-element.74.refs_5_) | copy-start | bytes 36868
  4.0 11.5 %copy-start.38 = (s32[8,384]{1,0:T(8,128)}, s32[8,384]{1,0:T(8,128)S(1)}, u32[]{:S(2)}) copy-start(s32[8,384]{1,0:T(8,128)S(1)} %get-tuple-element.117.refs_27_) | copy-start | bytes 36868
  4.0 11.5 %copy-start.40 = (s32[8,384]{1,0:T(8,128)}, s32[8,384]{1,0:T(8,128)S(1)}, u32[]{:S(2)}) copy-start(s32[8,384]{1,0:T(8,128)S(1)} %get-tuple-element.65.order_ref) | copy-start | bytes 36868
  15.5 39.1 %all-to-all-start.1 = ((s32[8,8,128]{2,1,0:T(8,128)}), s32[8,8,128]{2,1,0:T(8,128)}, u32[]{:S(2)}, u32[]{:S(2)}) async-start(s32[8,8,128]{2,1,0:T(8,128)} %get-tuple-element.62), calls=%async_computation.1 | async-start | bytes 65536 | tf_op jit(solution)/shard_map/all_to_all | solution.py:616
  25.5 1.2 copy-start.45
  26.6 1.0 copy-start.46
  27.7 1.1 copy-start.17
  27.7 1.1 copy-start.41
  54.6 1.0 copy-start.1
  59.5 9.6 %copy-start.24 = (f32[8,1,7,8,128]{4,3,2,1,0:T(8,128)}, f32[8,1,7,8,128]{4,3,2,1,0:T(8,128)S(1)}, u32[]{:S(2)}) copy-start(f32[8,1,7,8,128]{4,3,2,1,0:T(8,128)S(1)} %get-tuple-element.71) | copy-start | bytes 688132
  59.5 9.6 %copy-start.34 = (s32[8,128]{1,0:T(8,128)}, s32[8,128]{1,0:T(8,128)S(1)}, u32[]{:S(2)}) copy-start(s32[8,128]{1,0:T(8,128)S(1)} %get-tuple-element.84.refs_22_.refs_23_.refs_25_) | copy-start | bytes 12292
  69.2 13.6 %all-to-all-start.3 = ((f32[8,1,7,8,128]{4,3,2,1,0:T(8,128)}), f32[8,1,7,8,128]{4,3,2,1,0:T(8,128)}, u32[]{:S(2)}, u32[]{:S(2)}) async-start(f32[8,1,7,8,128]{4,3,2,1,0:T(8,128)} %copy-done.24), calls=%async_computation.3 | async-start | bytes 458752 | tf_op jit(solution)/shard_map/all_to_all | solution.py:616
  83.5 1.0 copy-start.2
  84.5 1.0 copy-start.6
  85.5 1.0 copy-start.8
  107.5 28.6 %copy-start.14 = (f32[9,56,128]{2,1,0:T(8,128)S(1)}, f32[9,56,128]{2,1,0:T(8,128)}, u32[]{:S(2)}) copy-start(f32[9,56,128]{2,1,0:T(8,128)} %get-tuple-element.121.refs_13_) | copy-start | bytes 774148
  107.6 28.6 %copy-start.23 = (f32[9,56,128]{2,1,0:T(8,128)S(1)}, f32[9,56,128]{2,1,0:T(8,128)}, u32[]{:S(2)}) copy-start(f32[9,56,128]{2,1,0:T(8,128)} %copy-done.22) | copy-start | bytes 774148
  119.6 16.5 %copy-start.4 = (f32[9,96,128]{2,1,0:T(8,128)S(1)}, f32[9,96,128]{2,1,0:T(8,128)}, u32[]{:S(2)}) copy-start(f32[9,96,128]{2,1,0:T(8,128)} %copy-done.3) | copy-start | bytes 1327108
  119.6 16.5 %copy-start.9 = (f32[9,96,128]{2,1,0:T(8,128)S(1)}, f32[9,96,128]{2,1,0:T(8,128)}, u32[]{:S(2)}) copy-start(f32[9,96,128]{2,1,0:T(8,128)} %copy-done.7) | copy-start | bytes 1327108
  161.4 23.5 %copy-start.11 = (f32[9,96,128]{2,1,0:T(8,128)S(1)}, f32[9,96,128]{2,1,0:T(8,128)}, u32[]{:S(2)}) copy-start(f32[9,96,128]{2,1,0:T(8,128)} %copy-done.10) | copy-start | bytes 1327108
  217.7 18.9 %copy-start.12 = (f32[9,56,128]{2,1,0:T(8,128)S(1)}, f32[9,56,128]{2,1,0:T(8,128)}, u32[]{:S(2)}) copy-start(f32[9,56,128]{2,1,0:T(8,128)} %get-tuple-element.120.refs_14_) | copy-start | bytes 774148
  217.7 19.0 %copy-start.19 = (f32[9,56,128]{2,1,0:T(8,128)S(1)}, f32[9,56,128]{2,1,0:T(8,128)}, u32[]{:S(2)}) copy-start(f32[9,56,128]{2,1,0:T(8,128)} %copy-done.18) | copy-start | bytes 774148
  (27 other events, 21.2 us)

commit v2 on v1

--- a/solution.py
+++ b/solution.py
@@ -22,6 +22,11 @@
 KROWS = 3 * B
 WROWS = KROWS + 4 * FP
 MSG = 7
+HALF = 224
+TROWS = Q * FP
+SOURCES = 12
+NEIGH = 4
+STAR = 8
 F32 = jnp.float32
 BF16 = jnp.bfloat16
 I32 = jnp.int32
@@ -30,16 +35,6 @@
 
 def shape(dims, dtype=F32):
     return jax.ShapeDtypeStruct(dims, dtype)
-
-
-def call(kernel, outs, scratch, name):
-    return pl.pallas_call(
-        kernel,
-        out_shape=outs,
-        scratch_shapes=scratch,
-        compiler_params=pltpu.CompilerParams(vmem_limit_bytes=VMEM_LIMIT),
-        name=name,
-    )
 
 
 def lane_take(x, index):
@@ -114,18 +109,18 @@
     return groups
 
 
-def row_bcast(ref, at, q):
-    return ref[at, pl.ds(q, 8, stride=0), :][None]
-
-
-def star_mix(star_ref, moved_ref, put):
+def row_bcast(ref, at, row):
+    return jnp.broadcast_to(ref[at, pl.ds(row, 1), :], (8, L))[None]
+
+
+def star_mix(mats_ref, moved_ref, put):
     for r0, rn in mix_groups(B, 32):
         acc = [None] * Q
         for d in range(3):
             for q in range(Q):
                 m = moved_ref[q, d * B + r0 : d * B + r0 + rn, :].reshape(rn // 8, 8, L)
                 for p in range(Q):
-                    term = row_bcast(star_ref, d * Q + p, q) * m
+                    term = row_bcast(mats_ref, p * Q + q, STAR + d) * m
                     acc[p] = term if acc[p] is None else acc[p] + term
         for p in range(Q):
             put(p, r0, rn, acc[p].reshape(rn, L))
@@ -141,7 +136,7 @@
 
 def index_kernel(
     dev_ref, label_ref, nbr_ref, face_ref, orient_ref, send_ref, stiff_ref, proj_ref, omap_ref,
-    order_ref, rank_ref, code_ref, lane_ref, sorted_orient_ref, send_blk_ref, send_lane_ref,
+    order_ref, rank_ref, near_ref, sorted_orient_ref, send_ref_out,
     req_a_ref, req_b_ref, w_ref, ow_ref, lw_ref,
     wf_ref, owf_ref, lwf_ref,
 ):
@@ -209,8 +204,7 @@
         slot = jnp.where(ghost, nbr - n_el, 0)
         peer = ((slot >> 5) * 11) >> 5
         slot = peer * SLOTS + (slot & 31)
-        code_ref[c] = jnp.where(ghost, 12 + (slot >> 7), face * 3 + (place >> 7))
-        lane_ref[c] = jnp.where(ghost, slot & 127, place & 127)
+        near_ref[c] = jnp.where(ghost, SOURCES * L + slot, face * (3 * L) + place)
         sorted_orient_ref[c] = orient
         slot = jnp.where(ghost, slot, -1)
         want = jnp.zeros((8, 2 * L), F32)
@@ -244,11 +238,10 @@
 
     send = jnp.maximum(send_ref[...], 0)
     place = pick(rank_blocks, send >> 7, send & 127)
-    send_blk_ref[...] = place >> 7
-    send_lane_ref[...] = place & 127
-
-
-def run_steps(count, star_ref, d_ref, w_ref, stack_ref, moved_ref):
+    send_ref_out[...] = place
+
+
+def run_steps(count, mats_ref, d_ref, w_ref, stack_ref, moved_ref):
     def body(k, carry):
         for q in range(Q):
             put_stack(stack_ref, q, d_ref[k, q], 64)
@@ -261,7 +254,7 @@
         def put(p, r0, rn, value):
             d_ref[k + 1, p, r0 : r0 + rn, :] = value
 
-        star_mix(star_ref, moved_ref, put)
+        star_mix(mats_ref, moved_ref, put)
         return carry
 
     lax.fori_loop(0, count, body, 0)
@@ -308,36 +301,54 @@
     return [a, b, c, d]
 
 
-def tile_at(v, k):
-    t = MSG * k + v
-    return (t // 3, t % 3) if t < 3 * Q else None
-
-
-def pack(dev_ref, rows, req_ref, send_blk_ref, send_lane_ref, gat_ref, msg_ref, out_a_ref, out_b_ref):
+def one_hot(hot_ref, index_ref, at, count, rows):
+    for f in range(count):
+        index = index_ref[at + f : at + f + 1, :]
+        for k in range(0, rows, 2 * L):
+            row = lax.broadcasted_iota(I32, (2 * L, L), 0) + k
+            match = jnp.broadcast_to(index, (2 * L, L)) == row
+            hot_ref[k : k + 2 * L, f * L : (f + 1) * L] = match.astype(F32).astype(BF16)
+
+
+def stack_rows(ref, at, column, values):
+    hi, lo = split(values)
+    rows = values.shape[0]
+    cols = slice(column * L, (column + 1) * L)
+    ref[at : at + rows, cols] = hi
+    ref[HALF + at : HALF + at + rows, cols] = lo
+
+
+def stack_traces(lhs_ref, sources):
+    for b in range(3):
+        for j in range(4):
+            rows = slice(j * FP, (j + 1) * FP)
+            for q in range(0, Q - 1, 2):
+                two = jnp.concatenate([sources[b][q, rows, :], sources[b][q + 1, rows, :]], axis=0)
+                stack_rows(lhs_ref, q * FP, j * 3 + b, two)
+            stack_rows(lhs_ref, (Q - 1) * FP, j * 3 + b, sources[b][Q - 1, rows, :])
+
+
+def both(out):
+    return out[0:TROWS] + out[HALF : HALF + TROWS]
+
+
+def pack(dev_ref, rows, send_ref, hot_ref, gat_ref, msg_ref, out_a_ref, out_b_ref):
     place_in_group = dev_ref[0] % GROUP
     other_place = (place_in_group + REACH) % GROUP
     lane = lax.broadcasted_iota(I32, (8, L), 1)
-    for at, (g, sources) in enumerate(rows):
+    for at, (g, lhs_ref) in enumerate(rows):
+        one_hot(hot_ref, send_ref, 2 * g, 2, SOURCES * L)
+        out = jnp.dot(lhs_ref[...], hot_ref[0 : SOURCES * L, 0 : 2 * L], preferred_element_type=F32)
+        gat_ref[:, 0 : 2 * L] = both(out)
         for half in range(2):
-            row = 2 * g + half
-            code = req_ref[row : row + 1] * 3 + send_blk_ref[row : row + 1]
-            code = rows_of(code, FP)
-            index = rows_of(send_lane_ref[row : row + 1], FP)
-
-            def body(q, carry):
-                blocks = [sources[k % 3][q, (k // 3) * FP : (k // 3) * FP + FP, :] for k in range(12)]
-                gat_ref[q] = pick(blocks, code, index)
-                return carry
-
-            lax.fori_loop(0, Q, body, 0)
             for v in range(MSG):
                 four = []
                 for k in range(4):
-                    t = tile_at(v, k)
-                    if t is None:
+                    t = MSG * k + v
+                    if t < 3 * Q:
+                        four.append(gat_ref[8 * t : 8 * t + 8, class_lanes(half)])
+                    else:
                         four.append(jnp.zeros((8, L), F32))
-                    else:
-                        four.append(gat_ref[t[0], 8 * t[1] : 8 * t[1] + 8, :])
                 for k, value in enumerate(block_transpose(four, lane)):
                     msg_ref[4 * half + k, v] = value
         for p in range(PEERS):
@@ -353,7 +364,7 @@
                 out_b_ref[jnp.where(within, 0, other_place + OFFSETS[p]), at] = msg_ref[p]
 
 
-def unpack(dev_ref, at, got_a_ref, got_b_ref, ghost_ref):
+def unpack(dev_ref, at, got_a_ref, got_b_ref, gat_ref, ghost_ref):
     place_in_group = dev_ref[0] % GROUP
     other_place = (place_in_group + REACH) % GROUP
     lane = lax.broadcasted_iota(I32, (8, L), 1)
@@ -368,15 +379,15 @@
         for v in range(MSG):
             moved = block_transpose([found[k][v] for k in range(4)], lane)
             for k in range(4):
-                t = tile_at(v, k)
-                if t is not None:
-                    ghost_ref[half, t[0], 8 * t[1] : 8 * t[1] + 8, :] = moved[k]
+                t = MSG * k + v
+                if t < 3 * Q:
+                    gat_ref[8 * t : 8 * t + 8, class_lanes(half)] = moved[k]
+        stack_rows(ghost_ref, 0, half, gat_ref[:, class_lanes(half)])
 
 
 def correct(
-    state_ref, own_ref, sources, ghost_ref, code_ref, lane_ref, orient_ref, c,
-    star_ref, fl_ref, fn_ref, w_ref, ow_ref, lw_ref,
-    stack_ref, moved_ref, chosen_ref, cstack_ref, near_ref, flux_ref, fstack_ref, new_ref,
+    state_ref, own_ref, lhs_ref, ghost_ref, index_ref, orient_ref, mats_ref, w_ref, ow_ref, lw_ref,
+    stack_ref, moved_ref, hot_ref, gat_ref, cstack_ref, near_ref, flux_ref, fstack_ref, new_ref,
 ):
     for q in range(Q):
         put_stack(stack_ref, q, own_ref[q], 64)
@@ -389,21 +400,15 @@
     def put(p, r0, rn, value):
         new_ref[p, r0 : r0 + rn, :] = state_ref[p, r0 : r0 + rn, :] + value
 
-    star_mix(star_ref, moved_ref, put)
+    star_mix(mats_ref, moved_ref, put)
+    one_hot(hot_ref, index_ref, 0, 4, (SOURCES + 2) * L)
+    out = jnp.dot(lhs_ref[...], hot_ref[0 : SOURCES * L, :], preferred_element_type=F32)
+    out = out + jnp.dot(ghost_ref[...], hot_ref[SOURCES * L :, :], preferred_element_type=F32)
+    gat_ref[...] = both(out)
     for f in range(4):
-        code = rows_of(code_ref[c, f : f + 1, :], FP)
-        index = rows_of(lane_ref[c, f : f + 1, :], FP)
-
-        def body(q, carry):
-            blocks = [sources[k % 3][q, (k // 3) * FP : (k // 3) * FP + FP, :] for k in range(12)]
-            blocks += [ghost_ref[half, q] for half in range(2)]
-            chosen_ref[q] = pick(blocks, code, index)
-            return carry
-
-        lax.fori_loop(0, Q, body, 0)
         for q in range(Q):
-            put_stack(cstack_ref, q, chosen_ref[q], 32)
-        turn = rows_of(orient_ref[c, f : f + 1, :], FP)
+            put_stack(cstack_ref, q, gat_ref[q * FP : (q + 1) * FP, f * L : (f + 1) * L], 32)
+        turn = rows_of(orient_ref[f : f + 1, :], FP)
 
         def store_near(q, out):
             value = jnp.where(turn == 1, out[FP : 2 * FP], out[0:FP])
@@ -418,9 +423,9 @@
             mine = moved_ref[q, pl.ds(KROWS + r, FP), :].reshape(3, 8, L)
             theirs = near_ref[q, pl.ds(r, FP), :].reshape(3, 8, L)
             for p in range(Q):
-                term = row_bcast(fl_ref, f * Q + p, q) * mine
+                term = row_bcast(mats_ref, p * Q + q, f) * mine
                 acc[p] = term if acc[p] is None else acc[p] + term
-                acc[p] = acc[p] + row_bcast(fn_ref, f * Q + p, q) * theirs
+                acc[p] = acc[p] + row_bcast(mats_ref, p * Q + q, NEIGH + f) * theirs
         for p in range(Q):
             flux_ref[p, pl.ds(r, FP), :] = acc[p].reshape(FP, L)
         return carry
@@ -435,70 +440,11 @@
     product(lw_ref[...], fstack_ref, subtract, contract=0)
 
 
-def first_kernel(
-    state_ref, star_ref, fl_ref, fn_ref, order_ref, w_ref,
-    s_ref, star_out, fl_out, fn_out, own0, own1, own2, t00, t10, t11, t20, t21, t22, t23,
-    d_ref, stack_ref, moved_ref,
-):
-    picks = []
-    for c in range(3):
-        picks.append((order_ref[0:1, class_lanes(c)], order_ref[1:2, class_lanes(c)]))
-
-    def sort_rows(src, rows, put):
-        blocks = [src[:, class_lanes(b)] for b in range(3)]
-        for c in range(3):
-            put(c, pick(blocks, rows_of(picks[c][0], rows), rows_of(picks[c][1], rows)))
-
-    def sort_state(q, carry):
-        def put(c, value):
-            s_ref[c, q] = value
-            d_ref[c, 0, q] = value
-
-        sort_rows(state_ref[q], B, put)
-        return carry
-
-    lax.fori_loop(0, Q, sort_state, 0)
-
-    def sort_matrix(src, dst, at, i, p):
-        def put(c, value):
-            dst[c, at, 0:Q, :] = value
-
-        sort_rows(src[i, p], Q, put)
-
-    def sort_star(p, carry):
-        for d in range(3):
-            sort_matrix(star_ref, star_out, d * Q + p, d, p)
-        return carry
-
-    lax.fori_loop(0, Q, sort_star, 0)
-
-    def sort_flux(p, carry):
-        for f in range(4):
-            sort_matrix(fl_ref, fl_out, f * Q + p, f, p)
-            sort_matrix(fn_ref, fn_out, f * Q + p, f, p)
-        return carry
-
-    lax.fori_loop(0, Q, sort_flux, 0)
-
-    def each(c, carry):
-        run_steps(ORDER - 1, star_out.at[c], d_ref.at[c], w_ref, stack_ref, moved_ref)
-        return carry
-
-    lax.fori_loop(0, 3, each, 0)
-    after_steps(0, d_ref.at[0], w_ref, stack_ref, own0, [t00])
-    after_steps(1, d_ref.at[1], w_ref, stack_ref, own1, [t10, t11])
-    after_steps(2, d_ref.at[2], w_ref, stack_ref, own2, [t20, t21, t22, t23])
-
-
-def first_pack_kernel(
-    dev_ref, req_a_ref, req_b_ref, send_blk_ref, send_lane_ref, t0, t1, t2,
-    req_ref, out_a_ref, out_b_ref,
-    gat_ref, msg_ref,
-):
+def read_requests(dev_ref, req_a_ref, req_b_ref, place_ref, send_ref):
     place_in_group = dev_ref[0] % GROUP
     other_place = (place_in_group + REACH) % GROUP
     lane = lax.broadcasted_iota(I32, (1, L), 1)
-    rows = [jnp.zeros((1, L), I32) for _ in range(8)]
+    rows = [jnp.zeros((1, L), I32) for _ in range(6)]
     for p in range(PEERS):
         at_group = place_in_group + OFFSETS[p]
         within = jnp.logical_and(at_group >= 0, at_group < GROUP)
@@ -512,8 +458,68 @@
             row = 2 * g + p // 4
             rows[row] = jnp.where(part, message[g : g + 1], rows[row])
     for row in range(8):
-        req_ref[row : row + 1] = rows[row]
-    pack(dev_ref, [(0, [t0, t1, t2])], req_ref, send_blk_ref, send_lane_ref, gat_ref, msg_ref, out_a_ref, out_b_ref)
+        send_ref[row : row + 1] = rows[row % 6] * (3 * L) + place_ref[row : row + 1]
+
+
+def first_kernel(
+    dev_ref, req_a_ref, req_b_ref, place_ref, state_ref, star_ref, fl_ref, fn_ref, order_ref, w_ref,
+    s0, s1, s2, mats, own0, own1, own2, t00, t10, t11, t20, t21, t22, t23, send_ref, lhs_ref,
+    out_a_ref, out_b_ref,
+    d_ref, stack_ref, moved_ref, hot_ref, gat_ref, msg_ref,
+):
+    picks = []
+    for c in range(3):
+        picks.append((order_ref[0:1, class_lanes(c)], order_ref[1:2, class_lanes(c)]))
+    states = [s0, s1, s2]
+
+    def sort_rows(blocks, put):
+        rows = blocks[0].shape[0]
+        for c in range(3):
+            put(c, pick(blocks, rows_of(picks[c][0], rows), rows_of(picks[c][1], rows)))
+
+    def sort_state(q, carry):
+        def put(c, value):
+            states[c][q] = value
+            d_ref[c, 0, q] = value
+
+        sort_rows([state_ref[q, :, class_lanes(b)] for b in range(3)], put)
+        return carry
+
+    lax.fori_loop(0, Q, sort_state, 0)
+
+    def sort_matrices(p, carry):
+        for q in range(Q):
+            at = p * Q + q
+
+            def put_flux(c, value):
+                mats[c, at, 0:8, :] = value
+
+            def put_star(c, value):
+                mats[c, at, STAR : STAR + 3, :] = value
+
+            sort_rows(
+                [
+                    jnp.concatenate([fl_ref[p, q, :, class_lanes(b)], fn_ref[p, q, :, class_lanes(b)]], axis=0)
+                    for b in range(3)
+                ],
+                put_flux,
+            )
+            sort_rows([star_ref[p, q, :, class_lanes(b)] for b in range(3)], put_star)
+        return carry
+
+    lax.fori_loop(0, Q, sort_matrices, 0)
+
+    def each(c, carry):
+        run_steps(ORDER - 1, mats.at[c], d_ref.at[c], w_ref, stack_ref, moved_ref)
+        return carry
+
+    lax.fori_loop(0, 3, each, 0)
+    after_steps(0, d_ref.at[0], w_ref, stack_ref, own0, [t00])
+    after_steps(1, d_ref.at[1], w_ref, stack_ref, own1, [t10, t11])
+    after_steps(2, d_ref.at[2], w_ref, stack_ref, own2, [t20, t21, t22, t23])
+    read_requests(dev_ref, req_a_ref, req_b_ref, place_ref, send_ref)
+    stack_traces(lhs_ref, [t00, t10, t20])
+    pack(dev_ref, [(0, lhs_ref)], send_ref, hot_ref, gat_ref, msg_ref, out_a_ref, out_b_ref)
 
 
 def step_kernel(n, *refs):
@@ -527,11 +533,12 @@
     ending = [c for c in range(3) if n % 2**c == 0]
     sending = [c for c in range(3) if (n + 1) % 2**c == 0] if n < STEPS else []
     last = n == STEPS
-    (dev_ref, got_a, got_b, code_ref, lane_ref, orient_ref) = take(6)
-    star_ref, fl_ref, fn_ref, w_ref, ow_ref, lw_ref = take(6)
+    (dev_ref, got_a, got_b, index_ref, orient_ref) = take(5)
+    (mats,) = take(1)
+    w_ref, ow_ref, lw_ref = take(3)
     states = dict((c, take(1)[0]) for c in ending)
     owns = dict((c, take(1)[0]) for c in ending)
-    sources = dict((c, take(3)) for c in ending)
+    sources = dict((c, take(1)[0]) for c in ending)
     if last:
         (rank_ref,) = take(1)
         final_ref, energy_ref = take(2)
@@ -540,25 +547,27 @@
         kept = dict((c, take(1)[0]) for c in range(3) if c not in ending)
         before = take(3) if n % 2 == 1 else None
         half_sums = take(3) if n == 3 else None
-        req_ref, send_blk_ref, send_lane_ref = take(3)
+        (send_ref,) = take(1)
         news = dict((c, take(1)[0]) for c in ending)
         new_owns = dict((c, take(1)[0]) for c in ending)
         new_traces = dict((c, take(2**c)) for c in ending)
-        sums = take(3) if n % 2 == 1 else None
-        full_sums = take(3) if n == 3 else None
+        sums = take(3) if n == 1 else None
+        lhs = dict((c, take(1)[0]) for c in sending)
         out_a_ref, out_b_ref = take(2)
-    ghost_ref, stack_ref, moved_ref, chosen_ref, cstack_ref, near_ref, flux_ref, fstack_ref = take(8)
+    ghost_ref, stack_ref, moved_ref, hot_ref, gat_ref, cstack_ref, near_ref, flux_ref, fstack_ref = take(9)
     if last:
         (new_scratch,) = take(1)
         news = dict((c, new_scratch.at[c]) for c in range(3))
     else:
         d_ref, msg_ref = take(2)
+        if n == 3:
+            sums = take(3)
     for at, c in enumerate(ending):
-        unpack(dev_ref, at, got_a, got_b, ghost_ref)
+        unpack(dev_ref, at, got_a, got_b, gat_ref, ghost_ref)
         correct(
-            states[c], owns[c], sources[c], ghost_ref, code_ref, lane_ref, orient_ref, c,
-            star_ref.at[c], fl_ref.at[c], fn_ref.at[c], w_ref, ow_ref, lw_ref,
-            stack_ref, moved_ref, chosen_ref, cstack_ref, near_ref, flux_ref, fstack_ref, news[c],
+            states[c], owns[c], sources[c], ghost_ref, index_ref.at[c], orient_ref.at[c],
+            mats.at[c], w_ref, ow_ref, lw_ref,
+            stack_ref, moved_ref, hot_ref, gat_ref, cstack_ref, near_ref, flux_ref, fstack_ref, news[c],
         )
     if last:
         total = jnp.zeros((8, L), F32)
@@ -581,21 +590,21 @@
     for c in ending:
         for q in range(Q):
             d_ref[0, q] = news[c][q]
-        run_steps(ORDER - 1, star_ref.at[c], d_ref, w_ref, stack_ref, moved_ref)
+        run_steps(ORDER - 1, mats.at[c], d_ref, w_ref, stack_ref, moved_ref)
         after_steps(c, d_ref, w_ref, stack_ref, new_owns[c], new_traces[c])
     now = [new_traces[c][0] if c in ending else kept[c] for c in range(3)]
+    stack_traces(lhs[0], now)
     if sums is not None:
         for b in range(3):
             for q in range(Q):
-                value = before[b][q] + now[b][q]
-                sums[b][q] = value
-                if full_sums is not None:
-                    full_sums[b][q] = value + half_sums[b][q]
-    given = {0: now, 1: sums, 2: full_sums}
-    pack(
-        dev_ref, [(g, given[g]) for g in sending], req_ref, send_blk_ref, send_lane_ref,
-        chosen_ref, msg_ref, out_a_ref, out_b_ref,
-    )
+                sums[b][q] = before[b][q] + now[b][q]
+        stack_traces(lhs[1], sums)
+    if n == 3:
+        for b in range(3):
+            for q in range(Q):
+                sums[b][q] = sums[b][q] + half_sums[b][q]
+        stack_traces(lhs[2], sums)
+    pack(dev_ref, [(g, lhs[g]) for g in sending], send_ref, hot_ref, gat_ref, msg_ref, out_a_ref, out_b_ref)
 
 
 FIELD = (Q, B, L)
@@ -633,10 +642,10 @@
             name=name,
         )(*args)
 
-    (order, rank, code, lane, orient, send_blk, send_lane, req_a, req_b, w, ow, lw) = run(
+    (order, rank, near, orient, place, req_a, req_b, w, ow, lw) = run(
         index_kernel,
         [dev, class_label.reshape(1, elements), neighbor, neighbor_face, orientation, send, stiffness, face_proj, orient_map],
-        [shape((8, elements), I32)] * 2 + [shape((3, 8, L), I32)] * 3 + [shape((8, L), I32)] * 2
+        [shape((8, elements), I32)] * 2 + [shape((3, 8, L), I32)] * 2 + [shape((8, L), I32)]
         + [shape((GROUP, 8, L), I32)] * 2
         + [shape((WROWS, 192), BF16), shape((3 * FP, 96), BF16), shape((288, B), BF16)],
         [pltpu.VMEM((WROWS, 192), F32), pltpu.VMEM((3 * FP, 96), F32), pltpu.VMEM((288, B), F32)],
@@ -645,39 +654,39 @@
     got_req = exchange(req_a, req_b)
     stack = pltpu.VMEM((192, Q * L), BF16)
     moved = pltpu.VMEM((Q, WROWS, L), F32)
-    (sorted_state, star_s, fl_s, fn_s, own0, own1, own2, t00, t10, t11, t20, t21, t22, t23) = run(
-        first_kernel,
-        [state, star, flux_local, flux_neigh, order, w],
-        [shape((3,) + FIELD), shape((3, 27, 16, L)), shape((3, 36, 16, L)), shape((3, 36, 16, L))]
-        + [shape(FIELD)] * 3 + [shape(TRACE)] * 7,
-        [pltpu.VMEM((3, ORDER) + FIELD, F32), stack, moved],
-        "first",
-        with_dev=False,
+    hot = pltpu.VMEM(((SOURCES + 2) * L, 4 * L), BF16)
+    gat = pltpu.VMEM((TROWS, 4 * L), F32)
+    msg = pltpu.VMEM((PEERS, MSG, 8, L), F32)
+    stacked = shape((2 * HALF, SOURCES * L), BF16)
+
+    def matrices(array):
+        return array.transpose(1, 2, 0, 3)
+
+    got = list(
+        run(
+            first_kernel,
+            [dev, *got_req, place, state, matrices(star), matrices(flux_local), matrices(flux_neigh), order, w],
+            [shape(FIELD)] * 3 + [shape((3, Q * Q, 16, L))] + [shape(FIELD)] * 3 + [shape(TRACE)] * 7
+            + [shape((8, L), I32), stacked] + [shape((GROUP, 1, MSG, 8, L))] * 2,
+            [pltpu.VMEM((3, ORDER) + FIELD, F32), stack, moved, hot, gat, msg],
+            "first",
+        )
     )
-    gat = pltpu.VMEM((Q, FP, L), F32)
-    msg = pltpu.VMEM((PEERS, MSG, 8, L), F32)
-    req, out_a, out_b = run(
-        first_pack_kernel,
-        [dev, *got_req, send_blk, send_lane, t00, t10, t20],
-        [shape((8, L), I32)] + [shape((GROUP, 1, MSG, 8, L))] * 2,
-        [gat, msg],
-        "first_pack",
-    )
-    fields = [sorted_state[c] for c in range(3)]
-    owns = [own0, own1, own2]
+    fields = got[0:3]
+    mats = got[3]
+    owns = got[4:7]
+    t00, t10, t11, t20, t21, t22, t23, send_index, lhs, out_a, out_b = got[7:]
     later = {1: {0: t10, 1: t11}, 2: {0: t20, 1: t21, 2: t22, 3: t23}}
     now = [t00, t10, t20]
-    sources = {0: now}
+    sources = {0: lhs}
     half_sums = None
     for n in range(1, STEPS + 1):
         ending = [c for c in range(3) if n % 2**c == 0]
         got_a, got_b = exchange(out_a, out_b)
-        args = [dev, got_a, got_b, code, lane, orient, star_s, fl_s, fn_s, w, ow, lw]
-        args += [fields[c] for c in ending] + [owns[c] for c in ending]
-        for c in ending:
-            args += sources[c]
+        args = [dev, got_a, got_b, near, orient, mats, w, ow, lw]
+        args += [fields[c] for c in ending] + [owns[c] for c in ending] + [sources[c] for c in ending]
         common = [
-            pltpu.VMEM((2, Q, FP, L), F32), stack, moved, gat, pltpu.VMEM((96, Q * L), BF16),
+            pltpu.VMEM((2 * HALF, 2 * L), BF16), stack, moved, hot, gat, pltpu.VMEM((96, Q * L), BF16),
             pltpu.VMEM(TRACE, F32), pltpu.VMEM(TRACE, F32), pltpu.VMEM((288, Q * L), BF16),
         ]
 
@@ -700,11 +709,13 @@
             args += now
         if n == 3:
             args += half_sums
-        args += [req, send_blk, send_lane]
+        args += [send_index]
         outs = [shape(FIELD)] * (2 * len(ending)) + [shape(TRACE)] * sum(2**c for c in ending)
-        outs += [shape(TRACE)] * (3 if n % 2 == 1 else 0) + [shape(TRACE)] * (3 if n == 3 else 0)
+        outs += [shape(TRACE)] * (3 if n == 1 else 0) + [stacked] * len(sending)
         outs += [shape((GROUP, len(sending), MSG, 8, L))] * 2
-        got = list(run(kernel, args, outs, common + [pltpu.VMEM((ORDER,) + FIELD, F32), msg], "step%d" % n))
+        scratch = common + [pltpu.VMEM((ORDER,) + FIELD, F32), msg]
+        scratch += [pltpu.VMEM(TRACE, F32)] * (3 if n == 3 else 0)
+        got = list(run(kernel, args, outs, scratch, "step%d" % n))
         for c in ending:
             fields[c] = got.pop(0)
         for c in ending:
@@ -713,14 +724,10 @@
             made = [got.pop(0) for _ in range(2**c)]
             later[c] = dict(enumerate(made))
         now = [later[c][n % 2**c] for c in range(3)]
-        sources = {0: now}
-        if n % 2 == 1:
-            sums = [got.pop(0) for _ in range(3)]
-            sources[1] = sums
-            if n == 1:
-                half_sums = sums
-        if n == 3:
-            sources[2] = [got.pop(0) for _ in range(3)]
+        if n == 1:
+            half_sums = [got.pop(0) for _ in range(3)]
+        for c in sending:
+            sources[c] = got.pop(0)
         out_a, out_b = got
     spread = lax.all_to_all(energy_out, "dom", 0, 0, tiled=True)
     energy = jnp.sum(spread).reshape(1) / (devices * elements * Q * B)

time: 283 us -> 238 us (0.84)
  Pallas kernels: 107 us -> 74.3 us
  blocking collectives: 124 us -> 149 us
  starting transfers between devices: 19.6 us -> 0 us
  local copies, waits for them, and re-layouts: 25.2 us -> 10.3 us
    pallas_call x7 -> x6, Pallas kernels: 107 us -> 74.3 us  [run(): pl.pallas_call(kernel, in_specs=[smem if with_dev and i == 0 else whole f...]
    all_to_all x3 -> x5, blocking collectives: 49.4 us -> 74.3 us  [exchange(): lax.all_to_all(second, 'dom', 0, 0, axis_index_groups=shifted, tiled=True)]
    all_to_all x2 -> x0, starting transfers between devices: 19.6 us -> none  [exchange(): lax.all_to_all(second, 'dom', 0, 0, axis_index_groups=shifted, tiled=True)]
    unnamed x102 -> x19, local copies, waits for them, and re-layouts: 22.1 us -> 8.74 us
  transfers between devices with their start and end apart: 2 -> 0, of which waited for: 1 -> 0; matrix products, arithmetic and copies ran while one was open for 1% -> 0% of each run, Pallas kernels for 7% -> 0%
where the time goes in v2:
time: 238 us; the launch traced here: 237 us
  blocking collectives  149 us (63%)
  Pallas kernels  74.3 us (31%)
  local copies, waits for them, and re-layouts  10.3 us (4%)
  between operations  2.47 us (1%)
    pallas_call x6, Pallas kernels, run(): pl.pallas_call(kernel, in_specs=[smem if with_dev and i == 0 else whole f...  74.3 us
    all_to_all x5, blocking collectives, exchange(): lax.all_to_all(second, 'dom', 0, 0, axis_index_groups=shifted, tiled=True)  74.3 us
    all_to_all x5, blocking collectives, exchange(): lax.all_to_all(first, 'dom', 0, 0, axis_index_groups=aligned, tiled=True)  56.5 us
    all_to_all x1, blocking collectives, shards(): spread = lax.all_to_all(energy_out, 'dom', 0, 0, tiled=True)  18 us
    unnamed x19, local copies, waits for them, and re-layouts  8.74 us

profile of v2, /device:TPU:1, one launch (start us, length us, event | category | flops | bytes accessed | tf_op | source)
XLA Modules:
  0.0 236.7 jit_solution(11063562615517155935)
XLA Ops:
  2.2 0.8 copy.17.proj_ref
  3.0 0.9 copy-done.4
  3.9 0.8 copy-done.5
  6.8 1.1 index.1
  7.9 11.3 %all_to_all.55.req_a_ref = s32[8,8,128]{2,1,0:T(8,128)S(1)} all-to-all(s32[8,8,128]{2,1,0:T(8,128)S(1)} %get-tuple-element.58), channel_id=1, replica_groups={{0,1,2,3,4,5,6,7},{8,9,10,11,12,13,14,15},{16,17,18,19,20,21,22,23},{24..., dimensions={0} | all-to-all | bytes 65536 | tf_op jit(solution)/shard_map/all_to_all | solution.py:624
  19.2 11.2 %all_to_all.56.req_b_ref = s32[8,8,128]{2,1,0:T(8,128)S(1)} all-to-all(s32[8,8,128]{2,1,0:T(8,128)S(1)} %get-tuple-element.59), channel_id=1, replica_groups={{4,5,6,7,8,9,10,11},{12,13,14,15,16,17,18,19},{20,21,22,23,24,25,26,27}..., dimensions={0} | all-to-all | bytes 65536 | tf_op jit(solution)/shard_map/all_to_all | solution.py:625
  30.4 1.1 copy-done
  31.5 1.0 copy-done.1
  32.5 1.0 copy-done.2
  33.6 1.0 copy-done.3
  34.6 19.5 %first.1 = (f32[9,56,128]{2,1,0:T(8,128)S(1)}, f32[9,56,128]{2,1,0:T(8,128)S(1)}, f32[9,56,128]{2,1,0:T(8,128)S(1)}, f32[3,81,16,128]{3,2,1,0:T(8,128)S(1)}, f32...) custom-call(s32[1]{0:T(128)} %bitcast.dev_ref.refs_0_, ...), custom_call_target="tpu_custom_call" | custom-call | tf_op jit(solution)/shard_map/first/pallas_call | solution.py:635
  54.1 9.5 %all_to_all.57.refs_1_ = f32[8,1,7,8,128]{4,3,2,1,0:T(8,128)S(1)} all-to-all(f32[8,1,7,8,128]{4,3,2,1,0:T(8,128)S(1)} %get-tuple-element.63), channel_id=1, replica_groups={{0,1,2,3,4,5,6,7},{8,9,10,11,12,13,14,15},{16,17,18,19,20,21,22,23},{24..., dimensions={0} | all-to-all | bytes 458752 | tf_op jit(solution)/shard_map/all_to_all | solution.py:624
  63.6 13.9 %all_to_all.58.refs_2_ = f32[8,1,7,8,128]{4,3,2,1,0:T(8,128)S(1)} all-to-all(f32[8,1,7,8,128]{4,3,2,1,0:T(8,128)S(1)} %get-tuple-element.64), channel_id=1, replica_groups={{4,5,6,7,8,9,10,11},{12,13,14,15,16,17,18,19},{20,21,22,23,24,25,26,27}..., dimensions={0} | all-to-all | bytes 458752 | tf_op jit(solution)/shard_map/all_to_all | solution.py:625
  77.5 11.2 %step1.1 = (f32[9,56,128]{2,1,0:T(8,128)S(1)}, f32[9,56,128]{2,1,0:T(8,128)S(1)}, f32[9,96,128]{2,1,0:T(8,128)}, f32[9,96,128]{2,1,0:T(8,128)S(1)}, f32[9,96,128...) custom-call(s32[1]{0:T(128)} %bitcast.dev_ref.refs_0_, ...), custom_call_target="tpu_custom_call" | custom-call | tf_op jit(solution)/shard_map/step1/pallas_call | solution.py:635
  88.8 11.9 %all_to_all.59.refs_1_ = f32[8,2,7,8,128]{4,3,2,1,0:T(8,128)S(1)} all-to-all(f32[8,2,7,8,128]{4,3,2,1,0:T(8,128)S(1)} %get-tuple-element.79), channel_id=1, replica_groups={{0,1,2,3,4,5,6,7},{8,9,10,11,12,13,14,15},{16,17,18,19,20,21,22,23},{24..., dimensions={0} | all-to-all | bytes 917504 | tf_op jit(solution)/shard_map/all_to_all | solution.py:624
  100.7 16.4 %all_to_all.60.refs_2_ = f32[8,2,7,8,128]{4,3,2,1,0:T(8,128)S(1)} all-to-all(f32[8,2,7,8,128]{4,3,2,1,0:T(8,128)S(1)} %get-tuple-element.80), channel_id=1, replica_groups={{4,5,6,7,8,9,10,11},{12,13,14,15,16,17,18,19},{20,21,22,23,24,25,26,27}..., dimensions={0} | all-to-all | bytes 917504 | tf_op jit(solution)/shard_map/all_to_all | solution.py:625
  117.1 16.6 %step2.1 = (f32[9,56,128]{2,1,0:T(8,128)S(1)}, f32[9,56,128]{2,1,0:T(8,128)S(1)}, f32[9,56,128]{2,1,0:T(8,128)S(1)}, f32[9,56,128]{2,1,0:T(8,128)S(1)}, f32[9,96...) custom-call(s32[1]{0:T(128)} %bitcast.dev_ref.refs_0_, ...), custom_call_target="tpu_custom_call" | custom-call | tf_op jit(solution)/shard_map/step2/pallas_call | solution.py:635
  133.7 9.4 %all_to_all.61.refs_1_ = f32[8,1,7,8,128]{4,3,2,1,0:T(8,128)S(1)} all-to-all(f32[8,1,7,8,128]{4,3,2,1,0:T(8,128)S(1)} %get-tuple-element.88), channel_id=1, replica_groups={{0,1,2,3,4,5,6,7},{8,9,10,11,12,13,14,15},{16,17,18,19,20,21,22,23},{24..., dimensions={0} | all-to-all | bytes 458752 | tf_op jit(solution)/shard_map/all_to_all | solution.py:624
  143.1 14.0 %all_to_all.62.refs_2_ = f32[8,1,7,8,128]{4,3,2,1,0:T(8,128)S(1)} all-to-all(f32[8,1,7,8,128]{4,3,2,1,0:T(8,128)S(1)} %get-tuple-element.89), channel_id=1, replica_groups={{4,5,6,7,8,9,10,11},{12,13,14,15,16,17,18,19},{20,21,22,23,24,25,26,27}..., dimensions={0} | all-to-all | bytes 458752 | tf_op jit(solution)/shard_map/all_to_all | solution.py:625
  157.1 12.5 %step3.1 = (f32[9,56,128]{2,1,0:T(8,128)S(1)}, f32[9,56,128]{2,1,0:T(8,128)S(1)}, f32[9,96,128]{2,1,0:T(8,128)}, bf16[448,1536]{1,0:T(8,128)(2,1)S(1)}, bf16[448...) custom-call(s32[1]{0:T(128)} %bitcast.dev_ref.refs_0_, ...), custom_call_target="tpu_custom_call" | custom-call | tf_op jit(solution)/shard_map/step3/pallas_call | solution.py:635
  169.6 14.4 %all_to_all.63.refs_1_ = f32[8,3,7,8,128]{4,3,2,1,0:T(8,128)S(1)} all-to-all(f32[8,3,7,8,128]{4,3,2,1,0:T(8,128)S(1)} %get-tuple-element.100), channel_id=1, replica_groups={{0,1,2,3,4,5,6,7},{8,9,10,11,12,13,14,15},{16,17,18,19,20,21,22,23},{24..., dimensions={0} | all-to-all | bytes 1376256 | tf_op jit(solution)/shard_map/all_to_all | solution.py:624
  184.0 18.8 %all_to_all.64.refs_2_ = f32[8,3,7,8,128]{4,3,2,1,0:T(8,128)S(1)} all-to-all(f32[8,3,7,8,128]{4,3,2,1,0:T(8,128)S(1)} %get-tuple-element.101), channel_id=1, replica_groups={{4,5,6,7,8,9,10,11},{12,13,14,15,16,17,18,19},{20,21,22,23,24,25,26,27}..., dimensions={0} | all-to-all | bytes 1376256 | tf_op jit(solution)/shard_map/all_to_all | solution.py:625
  202.8 13.4 %last.1 = (f32[9,56,384]{2,1,0:T(8,128)}, f32[128,1,128]{2,1,0:T(1,128)S(1)}) custom-call(s32[1]{0:T(128)} %bitcast.dev_ref.refs_0_, f32[8,3,7,8,128]{4,3,2,1,0:T(8,128)S(1)} %all_to_all.63.refs_1_, f32[8,3,7,8,128]{4,3,2,1,0:T(8,128)S(1)} %all_to_all.64.refs_2_, s32[3,8,128]{2,1,0:T(8,128)S(1)} %get-tuple-element.65.refs_3_, ...), custom_call_target="tpu_custom_call" | custom-call | tf_op jit(solution)/shard_map/last/pallas_call | solution.py:635
  216.2 18.0 %all_to_all.65 = f32[128,1,128]{2,1,0:T(1,128)S(1)} all-to-all(f32[128,1,128]{2,1,0:T(1,128)S(1)} %get-tuple-element.113), channel_id=1, replica_groups=mesh['dom'=128] {'dom'}, dimensions={0} | all-to-all | bytes 131072 | tf_op jit(solution)/shard_map/all_to_all | solution.py:732
  (20 shorter events, 4.4 us)
Async XLA Ops:
  3.0 0.9 copy-start.4
  3.9 0.8 copy-start.5
  4.7 0.7 copy-start.6
  5.4 0.7 copy-start.7
  6.1 0.7 copy-start.8
  30.4 1.1 copy-start
  31.5 1.0 copy-start.1
  32.5 1.0 copy-start.2
  33.6 1.0 copy-start.3

commit v3 on v2

--- a/solution.py
+++ b/solution.py
@@ -23,6 +23,10 @@
 WROWS = KROWS + 4 * FP
 MSG = 7
 HALF = 224
+MSG0 = 16
+HALF0 = 512
+TILES = 3 * Q
+TILES0 = 7 * Q
 TROWS = Q * FP
 SOURCES = 12
 NEIGH = 4
@@ -134,13 +138,12 @@
     return lax.dot_general(a, b, (((1,), (1,)), ((), ())), preferred_element_type=F32)
 
 
-def index_kernel(
-    dev_ref, label_ref, nbr_ref, face_ref, orient_ref, send_ref, stiff_ref, proj_ref, omap_ref,
-    order_ref, rank_ref, near_ref, sorted_orient_ref, send_ref_out,
-    req_a_ref, req_b_ref, w_ref, ow_ref, lw_ref,
-    wf_ref, owf_ref, lwf_ref,
+def make_indices(
+    label_ref, nbr_ref, face_ref, orient_ref, send_ref, stiff_ref, proj_ref, omap_ref,
+    order_ref, rank_ref, near_ref, near_first_ref, sorted_orient_ref, place_ref, want_ref,
+    w_ref, ow_ref, lw_ref, wf_ref, owf_ref, lwf_ref, pad_ref,
 ):
-    n_el = label_ref.shape[1]
+    n_el = nbr_ref.shape[1]
     wf_ref[...] = jnp.zeros_like(wf_ref)
     owf_ref[...] = jnp.zeros_like(owf_ref)
     for d in range(3):
@@ -152,7 +155,7 @@
         wf_ref[rows, 128 : 128 + B] = k - hi
     lwf_ref[...] = jnp.zeros_like(lwf_ref)
     for j in range(4):
-        k = proj_ref[j]
+        k = proj_ref[:, j, :]
         hi = k.astype(BF16).astype(F32)
         rows = slice(KROWS + j * FP, KROWS + j * FP + FB)
         wf_ref[rows, 0:B] = hi
@@ -171,7 +174,7 @@
     w_ref[...] = wf_ref[...].astype(BF16)
     ow_ref[...] = owf_ref[...].astype(BF16)
     lw_ref[...] = lwf_ref[...].astype(BF16)
-    label = label_ref[...]
+    label = jnp.concatenate([label_ref[c : c + 1, :] for c in range(3)], axis=1)
     classes = lax.broadcasted_iota(I32, (8, n_el), 0)
     hot = (jnp.broadcast_to(label, (8, n_el)) == classes).astype(F32)
     row = lax.broadcasted_iota(I32, (n_el, n_el), 0)
@@ -190,8 +193,7 @@
     rank_blocks = [rows_of(rank[:, class_lanes(c)], 8) for c in range(3)]
     pad = jnp.zeros((4, n_el), I32)
     tables = [jnp.concatenate([ref[...], pad], axis=0) for ref in (nbr_ref, face_ref, orient_ref)]
-    sub = lax.broadcasted_iota(I32, (8, L), 0)
-    lanes = lax.broadcasted_iota(I32, (8, L), 1)
+    want_ref[...] = jnp.zeros_like(want_ref)
     for c in range(3):
         blk = rows_of(order[0:1, class_lanes(c)], 8)
         lane = rows_of(order[1:2, class_lanes(c)], 8)
@@ -206,6 +208,10 @@
         slot = peer * SLOTS + (slot & 31)
         near_ref[c] = jnp.where(ghost, SOURCES * L + slot, face * (3 * L) + place)
         sorted_orient_ref[c] = orient
+        if c == 0:
+            near_first_ref[...] = jnp.where(
+                ghost, SOURCES * L + face * (2 * L) + slot, face * (3 * L) + place
+            )
         slot = jnp.where(ghost, slot, -1)
         want = jnp.zeros((8, 2 * L), F32)
         target = lax.broadcasted_iota(I32, (2 * L, L), 0)
@@ -213,32 +219,22 @@
             match = (jnp.broadcast_to(slot[f : f + 1], (2 * L, L)) == target).astype(F32).astype(BF16)
             value = rows_of(face[f : f + 1], 8).astype(F32).astype(BF16)
             want = want + nt_dot(value, match)
-        want = want.astype(I32)
-        for p in range(PEERS):
-            half = want[:, class_lanes(p // 4)]
-            turn = (-(p % 4) * SLOTS) % L
-            moved = pltpu.roll(half, turn, axis=1) if turn else half
-            wf_ref[8 * p : 8 * p + 8, 0:L] = jnp.where(
-                sub == c, moved.astype(F32), wf_ref[8 * p : 8 * p + 8, 0:L]
-            )
-    place_in_group = dev_ref[0] % GROUP
-    other_place = (place_in_group + REACH) % GROUP
-    for p in range(PEERS):
-        message = wf_ref[8 * p : 8 * p + 8, 0:L].astype(I32)
-        to = place_in_group + OFFSETS[p]
-        within = jnp.logical_and(to >= 0, to < GROUP)
-
-        @pl.when(within)
-        def _():
-            req_a_ref[jnp.where(within, to, 0)] = message
-
-        @pl.when(jnp.logical_not(within))
-        def _():
-            req_b_ref[jnp.where(within, 0, other_place + OFFSETS[p])] = message
-
-    send = jnp.maximum(send_ref[...], 0)
-    place = pick(rank_blocks, send >> 7, send & 127)
-    send_ref_out[...] = place
+        want_ref[c : c + 1] = want[0:1]
+    pad_ref[...] = jnp.zeros_like(pad_ref)
+    pad_ref[:, 0:SLOTS] = jnp.maximum(send_ref[...], 0)
+    quarter = lax.broadcasted_iota(I32, (1, L), 1) >> 5
+    rows = []
+    for g in range(3):
+        for half in range(2):
+            row = jnp.zeros((1, L), I32)
+            for k in range(4):
+                r = 3 * (4 * half + k) + g
+                part = pad_ref[r : r + 1, :]
+                part = pltpu.roll(part, SLOTS * k, axis=1) if k else part
+                row = jnp.where(quarter == k, part, row)
+            rows.append(row)
+    send = jnp.concatenate(rows + rows[:2], axis=0)
+    place_ref[...] = pick(rank_blocks, send >> 7, send & 127)
 
 
 def run_steps(count, mats_ref, d_ref, w_ref, stack_ref, moved_ref):
@@ -310,79 +306,126 @@
             hot_ref[k : k + 2 * L, f * L : (f + 1) * L] = match.astype(F32).astype(BF16)
 
 
-def stack_rows(ref, at, column, values):
+def stack_rows(ref, at, column, values, apart=HALF):
     hi, lo = split(values)
     rows = values.shape[0]
     cols = slice(column * L, (column + 1) * L)
     ref[at : at + rows, cols] = hi
-    ref[HALF + at : HALF + at + rows, cols] = lo
+    ref[apart + at : apart + at + rows, cols] = lo
+
+
+def stack_quantities(lhs_ref, trace_ref, j, column):
+    rows = slice(j * FP, (j + 1) * FP)
+    for q in range(0, Q - 1, 2):
+        two = jnp.concatenate([trace_ref[q, rows, :], trace_ref[q + 1, rows, :]], axis=0)
+        stack_rows(lhs_ref, q * FP, column, two)
+    stack_rows(lhs_ref, (Q - 1) * FP, column, trace_ref[Q - 1, rows, :])
 
 
 def stack_traces(lhs_ref, sources):
     for b in range(3):
         for j in range(4):
-            rows = slice(j * FP, (j + 1) * FP)
-            for q in range(0, Q - 1, 2):
-                two = jnp.concatenate([sources[b][q, rows, :], sources[b][q + 1, rows, :]], axis=0)
-                stack_rows(lhs_ref, q * FP, j * 3 + b, two)
-            stack_rows(lhs_ref, (Q - 1) * FP, j * 3 + b, sources[b][Q - 1, rows, :])
+            stack_quantities(lhs_ref, sources[b], j, j * 3 + b)
 
 
 def both(out):
     return out[0:TROWS] + out[HALF : HALF + TROWS]
 
 
-def pack(dev_ref, rows, send_ref, hot_ref, gat_ref, msg_ref, out_a_ref, out_b_ref):
+def send_tiles(dev_ref, at, tile, count, msg_ref, out_ref, cross_ref):
     place_in_group = dev_ref[0] % GROUP
-    other_place = (place_in_group + REACH) % GROUP
     lane = lax.broadcasted_iota(I32, (8, L), 1)
+    for half in range(2):
+        for v in range(count):
+            four = [tile(count * k + v, half) for k in range(4)]
+            for k, value in enumerate(block_transpose(four, lane)):
+                msg_ref[4 * half + k, v] = value
+    for p in range(PEERS):
+        to = place_in_group + OFFSETS[p]
+        slot = (to + GROUP) % GROUP
+        if abs(OFFSETS[p]) < REACH:
+            out_ref[slot, at] = msg_ref[p]
+            continue
+        within = jnp.logical_and(to >= 0, to < GROUP)
+
+        @pl.when(within)
+        def _():
+            out_ref[slot, at] = msg_ref[p]
+
+        @pl.when(jnp.logical_not(within))
+        def _():
+            cross_ref[0, at] = msg_ref[p]
+
+
+def receive_tiles(dev_ref, at, count, got, put):
+    got_ref, cross_ref, far_ref = got
+    place_in_group = dev_ref[0] % GROUP
+    first = jnp.where(place_in_group < REACH, REACH + 1, 0)
+    lane = lax.broadcasted_iota(I32, (8, L), 1)
+    for half in range(2):
+        found = []
+        for k in range(4):
+            offset = OFFSETS[4 * half + k]
+            source = place_in_group + offset
+            within = jnp.logical_and(source >= 0, source < GROUP)
+            slot = (source + GROUP) % GROUP
+            near = got_ref[slot, at]
+            if abs(offset) == REACH:
+                other = cross_ref[0, at]
+            else:
+                other = far_ref[jnp.clip(slot - first, 0, REACH - 2), at]
+            found.append(jnp.where(within, near, other))
+        for v in range(count):
+            moved = block_transpose([found[k][v] for k in range(4)], lane)
+            for k in range(4):
+                put(count * k + v, half, moved[k])
+
+
+def pack(dev_ref, rows, send_ref, hot_ref, gat_ref, msg_ref, out_ref, cross_ref):
     for at, (g, lhs_ref) in enumerate(rows):
         one_hot(hot_ref, send_ref, 2 * g, 2, SOURCES * L)
         out = jnp.dot(lhs_ref[...], hot_ref[0 : SOURCES * L, 0 : 2 * L], preferred_element_type=F32)
         gat_ref[:, 0 : 2 * L] = both(out)
-        for half in range(2):
-            for v in range(MSG):
-                four = []
-                for k in range(4):
-                    t = MSG * k + v
-                    if t < 3 * Q:
-                        four.append(gat_ref[8 * t : 8 * t + 8, class_lanes(half)])
-                    else:
-                        four.append(jnp.zeros((8, L), F32))
-                for k, value in enumerate(block_transpose(four, lane)):
-                    msg_ref[4 * half + k, v] = value
-        for p in range(PEERS):
-            to = place_in_group + OFFSETS[p]
-            within = jnp.logical_and(to >= 0, to < GROUP)
-
-            @pl.when(within)
-            def _():
-                out_a_ref[jnp.where(within, to, 0), at] = msg_ref[p]
-
-            @pl.when(jnp.logical_not(within))
-            def _():
-                out_b_ref[jnp.where(within, 0, other_place + OFFSETS[p]), at] = msg_ref[p]
-
-
-def unpack(dev_ref, at, got_a_ref, got_b_ref, gat_ref, ghost_ref):
-    place_in_group = dev_ref[0] % GROUP
-    other_place = (place_in_group + REACH) % GROUP
-    lane = lax.broadcasted_iota(I32, (8, L), 1)
+
+        def tile(t, half):
+            if t < TILES:
+                return gat_ref[8 * t : 8 * t + 8, class_lanes(half)]
+            return jnp.zeros((8, L), F32)
+
+        send_tiles(dev_ref, at, tile, MSG, msg_ref, out_ref, cross_ref)
+
+
+def unpack(dev_ref, at, got, gat_ref, ghost_ref):
+    def put(t, half, value):
+        if t < TILES:
+            gat_ref[8 * t : 8 * t + 8, class_lanes(half)] = value
+
+    receive_tiles(dev_ref, at, MSG, got, put)
     for half in range(2):
-        found = []
-        for k in range(4):
-            at_group = place_in_group + OFFSETS[4 * half + k]
-            within = jnp.logical_and(at_group >= 0, at_group < GROUP)
-            first = got_a_ref[jnp.where(within, at_group, 0), at]
-            second = got_b_ref[jnp.where(within, 0, other_place + OFFSETS[4 * half + k]), at]
-            found.append(jnp.where(within, first, second))
-        for v in range(MSG):
-            moved = block_transpose([found[k][v] for k in range(4)], lane)
-            for k in range(4):
-                t = MSG * k + v
-                if t < 3 * Q:
-                    gat_ref[8 * t : 8 * t + 8, class_lanes(half)] = moved[k]
         stack_rows(ghost_ref, 0, half, gat_ref[:, class_lanes(half)])
+
+
+def unpack_first(dev_ref, got, place_ref, send_ref, whole_ref, w_ref, stack_ref, trace_ref, ghost_ref):
+    def put(t, half, value):
+        if t < TILES0:
+            whole_ref[half, t // 7, 8 * (t % 7) : 8 * (t % 7) + 8, :] = value
+            return
+        for g in range(3):
+            row = 2 * g + half
+            send_ref[row : row + 1] = value[g : g + 1].astype(I32) * (3 * L) + place_ref[row : row + 1]
+
+    receive_tiles(dev_ref, 0, MSG0, got, put)
+    send_ref[6:8] = place_ref[6:8]
+    for half in range(2):
+        for q in range(Q):
+            put_stack(stack_ref, q, whole_ref[half, q], 64)
+
+        def store(q, out):
+            trace_ref[q] = out
+
+        product(w_ref[KROWS:WROWS, :], stack_ref, store)
+        for j in range(4):
+            stack_quantities(ghost_ref, trace_ref, j, 2 * j + half)
 
 
 def correct(
@@ -401,9 +444,10 @@
         new_ref[p, r0 : r0 + rn, :] = state_ref[p, r0 : r0 + rn, :] + value
 
     star_mix(mats_ref, moved_ref, put)
-    one_hot(hot_ref, index_ref, 0, 4, (SOURCES + 2) * L)
+    ghosts = ghost_ref.shape[1]
+    one_hot(hot_ref, index_ref, 0, 4, SOURCES * L + ghosts)
     out = jnp.dot(lhs_ref[...], hot_ref[0 : SOURCES * L, :], preferred_element_type=F32)
-    out = out + jnp.dot(ghost_ref[...], hot_ref[SOURCES * L :, :], preferred_element_type=F32)
+    out = out + jnp.dot(ghost_ref[...], hot_ref[SOURCES * L : SOURCES * L + ghosts, :], preferred_element_type=F32)
     gat_ref[...] = both(out)
     for f in range(4):
         for q in range(Q):
@@ -440,33 +484,31 @@
     product(lw_ref[...], fstack_ref, subtract, contract=0)
 
 
-def read_requests(dev_ref, req_a_ref, req_b_ref, place_ref, send_ref):
-    place_in_group = dev_ref[0] % GROUP
-    other_place = (place_in_group + REACH) % GROUP
-    lane = lax.broadcasted_iota(I32, (1, L), 1)
-    rows = [jnp.zeros((1, L), I32) for _ in range(6)]
-    for p in range(PEERS):
-        at_group = place_in_group + OFFSETS[p]
-        within = jnp.logical_and(at_group >= 0, at_group < GROUP)
-        first = req_a_ref[jnp.where(within, at_group, 0)]
-        second = req_b_ref[jnp.where(within, 0, other_place + OFFSETS[p])]
-        message = jnp.where(within, first, second)
-        turn = (p % 4) * SLOTS
-        message = pltpu.roll(message, turn, axis=1) if turn else message
-        part = (lane >> 5) == (p % 4)
-        for g in range(3):
-            row = 2 * g + p // 4
-            rows[row] = jnp.where(part, message[g : g + 1], rows[row])
-    for row in range(8):
-        send_ref[row : row + 1] = rows[row % 6] * (3 * L) + place_ref[row : row + 1]
-
-
-def first_kernel(
-    dev_ref, req_a_ref, req_b_ref, place_ref, state_ref, star_ref, fl_ref, fn_ref, order_ref, w_ref,
-    s0, s1, s2, mats, own0, own1, own2, t00, t10, t11, t20, t21, t22, t23, send_ref, lhs_ref,
-    out_a_ref, out_b_ref,
-    d_ref, stack_ref, moved_ref, hot_ref, gat_ref, msg_ref,
-):
+def first_kernel(*refs):
+    dev_ref = refs[0]
+    hbm = refs[1:13]
+    (
+        s0, s1, s2, mats, own0, own1, own2, t00, t10, t11, t20, t21, t22, t23, lhs_ref,
+        near_ref, near_first_ref, sorted_orient_ref, rank_ref, place_ref, w_ref, ow_ref, lw_ref,
+        out_ref, cross_ref,
+    ) = refs[13:38]
+    local = refs[38:50]
+    (
+        sems, order_ref, want_ref, wf_ref, owf_ref, lwf_ref, pad_ref,
+        d_ref, stack_ref, moved_ref, hot_ref, jl_ref, gat_ref, msg_ref,
+    ) = refs[50:]
+    copies = [pltpu.make_async_copy(a, b, sems.at[i]) for i, (a, b) in enumerate(zip(hbm, local))]
+    for copy in copies:
+        copy.start()
+    for copy in copies[:8]:
+        copy.wait()
+    make_indices(
+        *local[:8], order_ref, rank_ref, near_ref, near_first_ref, sorted_orient_ref, place_ref, want_ref,
+        w_ref, ow_ref, lw_ref, wf_ref, owf_ref, lwf_ref, pad_ref,
+    )
+    for copy in copies[8:]:
+        copy.wait()
+    state_ref, star_ref, fl_ref, fn_ref = local[8:]
     picks = []
     for c in range(3):
         picks.append((order_ref[0:1, class_lanes(c)], order_ref[1:2, class_lanes(c)]))
@@ -517,9 +559,21 @@
     after_steps(0, d_ref.at[0], w_ref, stack_ref, own0, [t00])
     after_steps(1, d_ref.at[1], w_ref, stack_ref, own1, [t10, t11])
     after_steps(2, d_ref.at[2], w_ref, stack_ref, own2, [t20, t21, t22, t23])
-    read_requests(dev_ref, req_a_ref, req_b_ref, place_ref, send_ref)
     stack_traces(lhs_ref, [t00, t10, t20])
-    pack(dev_ref, [(0, lhs_ref)], send_ref, hot_ref, gat_ref, msg_ref, out_a_ref, out_b_ref)
+    for c in range(3):
+        for q in range(0, Q, 2):
+            parts = [integrate(d_ref.at[c], r, 0, 1) for r in range(q, min(q + 2, Q))]
+            stack_rows(jl_ref, q * B, c, jnp.concatenate(parts, axis=0), HALF0)
+    one_hot(hot_ref, place_ref, 0, 2, 3 * L)
+    out = jnp.dot(jl_ref[...], hot_ref[0 : 3 * L, 0 : 2 * L], preferred_element_type=F32)
+    gat_ref[...] = out[0 : Q * B] + out[HALF0 : HALF0 + Q * B]
+
+    def tile(t, half):
+        if t < TILES0:
+            return gat_ref[8 * t : 8 * t + 8, class_lanes(half)]
+        return want_ref[:, class_lanes(half)]
+
+    send_tiles(dev_ref, 0, tile, MSG0, msg_ref, out_ref, cross_ref)
 
 
 def step_kernel(n, *refs):
@@ -533,7 +587,9 @@
     ending = [c for c in range(3) if n % 2**c == 0]
     sending = [c for c in range(3) if (n + 1) % 2**c == 0] if n < STEPS else []
     last = n == STEPS
-    (dev_ref, got_a, got_b, index_ref, orient_ref) = take(5)
+    (dev_ref,) = take(1)
+    got = take(3)
+    index_ref, orient_ref = take(2)
     (mats,) = take(1)
     w_ref, ow_ref, lw_ref = take(3)
     states = dict((c, take(1)[0]) for c in ending)
@@ -547,13 +603,16 @@
         kept = dict((c, take(1)[0]) for c in range(3) if c not in ending)
         before = take(3) if n % 2 == 1 else None
         half_sums = take(3) if n == 3 else None
-        (send_ref,) = take(1)
+        near_first_ref, place_ref = take(2) if n == 1 else (None, None)
+        send_ref = take(1)[0] if n > 1 else None
         news = dict((c, take(1)[0]) for c in ending)
         new_owns = dict((c, take(1)[0]) for c in ending)
         new_traces = dict((c, take(2**c)) for c in ending)
         sums = take(3) if n == 1 else None
         lhs = dict((c, take(1)[0]) for c in sending)
-        out_a_ref, out_b_ref = take(2)
+        if n == 1:
+            (send_ref,) = take(1)
+        out_ref, cross_ref = take(2)
     ghost_ref, stack_ref, moved_ref, hot_ref, gat_ref, cstack_ref, near_ref, flux_ref, fstack_ref = take(9)
     if last:
         (new_scratch,) = take(1)
@@ -562,10 +621,17 @@
         d_ref, msg_ref = take(2)
         if n == 3:
             sums = take(3)
+        if n == 1:
+            (whole_ref,) = take(1)
     for at, c in enumerate(ending):
-        unpack(dev_ref, at, got_a, got_b, gat_ref, ghost_ref)
+        if n == 1:
+            unpack_first(
+                dev_ref, got, place_ref, send_ref, whole_ref, w_ref, stack_ref, near_ref, ghost_ref
+            )
+        else:
+            unpack(dev_ref, at, got, gat_ref.at[:, 0 : 2 * L], ghost_ref)
         correct(
-            states[c], owns[c], sources[c], ghost_ref, index_ref.at[c], orient_ref.at[c],
+            states[c], owns[c], sources[c], ghost_ref, near_first_ref if n == 1 else index_ref.at[c], orient_ref.at[c],
             mats.at[c], w_ref, ow_ref, lw_ref,
             stack_ref, moved_ref, hot_ref, gat_ref, cstack_ref, near_ref, flux_ref, fstack_ref, news[c],
         )
@@ -604,7 +670,7 @@
             for q in range(Q):
                 sums[b][q] = sums[b][q] + half_sums[b][q]
         stack_traces(lhs[2], sums)
-    pack(dev_ref, [(g, lhs[g]) for g in sending], send_ref, hot_ref, gat_ref, msg_ref, out_a_ref, out_b_ref)
+    pack(dev_ref, [(g, lhs[g]) for g in sending], send_ref, hot_ref, gat_ref, msg_ref, out_ref, cross_ref)
 
 
 FIELD = (Q, B, L)
@@ -618,23 +684,27 @@
     elements = state.shape[2]
     devices = lax.axis_size("dom")
     aligned = [[GROUP * k + i for i in range(GROUP)] for k in range(devices // GROUP)]
-    shifted = [[(m + REACH) % devices for m in group] for group in aligned]
-
-    def exchange(first, second):
-        got_a = lax.all_to_all(first, "dom", 0, 0, axis_index_groups=aligned, tiled=True)
-        got_b = lax.all_to_all(second, "dom", 0, 0, axis_index_groups=shifted, tiled=True)
-        return got_a, got_b
-
-    dev = lax.axis_index("dom").astype(I32).reshape(1)
-    send = send_list.reshape(2, 4, 3, SLOTS).transpose(2, 0, 1, 3).reshape(6, L)
-    send = jnp.concatenate([send, send[:2]], axis=0)
+    across = [(d, (d - REACH if d % GROUP < REACH else d + REACH) % devices) for d in range(devices)]
+    onward = [(d, (d + GROUP if d % GROUP < REACH else d - GROUP) % devices) for d in range(devices)]
+    axis_index = lax.axis_index("dom").astype(I32)
+    exit_first = jnp.where(axis_index % GROUP < REACH, REACH + 1, 0).astype(I32)
+    axis_index, exit_first = lax.optimization_barrier((axis_index, exit_first))
+
+    def exchange(out, cross):
+        got_cross = lax.ppermute(cross, "dom", across)
+        got = lax.all_to_all(out, "dom", 0, 0, axis_index_groups=aligned, tiled=True)
+        far = lax.dynamic_slice_in_dim(got, exit_first, REACH - 1, 0, allow_negative_indices=False)
+        return got, got_cross, lax.ppermute(far, "dom", onward)
+
+    dev = axis_index.reshape(1)
     smem = pl.BlockSpec(memory_space=pltpu.SMEM)
     whole = pl.BlockSpec(memory_space=pltpu.VMEM)
-
-    def run(kernel, args, outs, scratch, name, with_dev=True):
+    stay = pl.BlockSpec(memory_space=pltpu.HBM)
+
+    def run(kernel, args, outs, scratch, name, rest=whole):
         return pl.pallas_call(
             kernel,
-            in_specs=[smem if with_dev and i == 0 else whole for i in range(len(args))],
+            in_specs=[smem] + [rest] * (len(args) - 1),
             out_specs=[whole] * len(outs),
             out_shape=outs,
             scratch_shapes=scratch,
@@ -642,51 +712,64 @@
             name=name,
         )(*args)
 
-    (order, rank, near, orient, place, req_a, req_b, w, ow, lw) = run(
-        index_kernel,
-        [dev, class_label.reshape(1, elements), neighbor, neighbor_face, orientation, send, stiffness, face_proj, orient_map],
-        [shape((8, elements), I32)] * 2 + [shape((3, 8, L), I32)] * 2 + [shape((8, L), I32)]
-        + [shape((GROUP, 8, L), I32)] * 2
-        + [shape((WROWS, 192), BF16), shape((3 * FP, 96), BF16), shape((288, B), BF16)],
-        [pltpu.VMEM((WROWS, 192), F32), pltpu.VMEM((3 * FP, 96), F32), pltpu.VMEM((288, B), F32)],
-        "index",
-    )
-    got_req = exchange(req_a, req_b)
     stack = pltpu.VMEM((192, Q * L), BF16)
     moved = pltpu.VMEM((Q, WROWS, L), F32)
-    hot = pltpu.VMEM(((SOURCES + 2) * L, 4 * L), BF16)
     gat = pltpu.VMEM((TROWS, 4 * L), F32)
-    msg = pltpu.VMEM((PEERS, MSG, 8, L), F32)
     stacked = shape((2 * HALF, SOURCES * L), BF16)
+
+    def hot(ghosts):
+        return pltpu.VMEM(((SOURCES + ghosts) * L, 4 * L), BF16)
+
+    def msg(count):
+        return pltpu.VMEM((PEERS, count, 8, L), F32)
+
+    def messages(rows, count):
+        return [shape((GROUP, rows, count, 8, L)), shape((1, rows, count, 8, L))]
 
     def matrices(array):
         return array.transpose(1, 2, 0, 3)
 
+    inputs = [
+        class_label.reshape(3, L), neighbor, neighbor_face, orientation, send_list, stiffness,
+        face_proj.transpose(1, 0, 2), orient_map,
+        state, matrices(star), matrices(flux_local), matrices(flux_neigh),
+    ]
     got = list(
         run(
             first_kernel,
-            [dev, *got_req, place, state, matrices(star), matrices(flux_local), matrices(flux_neigh), order, w],
-            [shape(FIELD)] * 3 + [shape((3, Q * Q, 16, L))] + [shape(FIELD)] * 3 + [shape(TRACE)] * 7
-            + [shape((8, L), I32), stacked] + [shape((GROUP, 1, MSG, 8, L))] * 2,
-            [pltpu.VMEM((3, ORDER) + FIELD, F32), stack, moved, hot, gat, msg],
+            [dev] + inputs,
+            [shape(FIELD)] * 3 + [shape((3, Q * Q, 16, L))] + [shape(FIELD)] * 3 + [shape(TRACE)] * 7 + [stacked]
+            + [shape((3, 8, L), I32), shape((8, L), I32), shape((3, 8, L), I32), shape((8, elements), I32), shape((8, L), I32)]
+            + [shape((WROWS, 192), BF16), shape((3 * FP, 96), BF16), shape((288, B), BF16)]
+            + messages(1, MSG0),
+            [pltpu.VMEM(x.shape, x.dtype) for x in inputs]
+            + [
+                pltpu.SemaphoreType.DMA((len(inputs),)),
+                pltpu.VMEM((8, elements), I32), pltpu.VMEM((8, 2 * L), F32),
+                pltpu.VMEM((WROWS, 192), F32), pltpu.VMEM((3 * FP, 96), F32), pltpu.VMEM((288, B), F32),
+                pltpu.VMEM((3 * PEERS, L), I32),
+                pltpu.VMEM((3, ORDER) + FIELD, F32), stack, moved, pltpu.VMEM((4 * L, 2 * L), BF16),
+                pltpu.VMEM((2 * HALF0, 3 * L), BF16), pltpu.VMEM((Q * B, 2 * L), F32), msg(MSG0),
+            ],
             "first",
+            rest=stay,
         )
     )
     fields = got[0:3]
     mats = got[3]
     owns = got[4:7]
-    t00, t10, t11, t20, t21, t22, t23, send_index, lhs, out_a, out_b = got[7:]
+    t00, t10, t11, t20, t21, t22, t23, lhs = got[7:15]
+    near, near_first, orient, rank, place, w, ow, lw, out, cross = got[15:]
     later = {1: {0: t10, 1: t11}, 2: {0: t20, 1: t21, 2: t22, 3: t23}}
     now = [t00, t10, t20]
     sources = {0: lhs}
     half_sums = None
     for n in range(1, STEPS + 1):
         ending = [c for c in range(3) if n % 2**c == 0]
-        got_a, got_b = exchange(out_a, out_b)
-        args = [dev, got_a, got_b, near, orient, mats, w, ow, lw]
+        args = [dev, *exchange(out, cross), near, orient, mats, w, ow, lw]
         args += [fields[c] for c in ending] + [owns[c] for c in ending] + [sources[c] for c in ending]
         common = [
-            pltpu.VMEM((2 * HALF, 2 * L), BF16), stack, moved, hot, gat, pltpu.VMEM((96, Q * L), BF16),
+            pltpu.VMEM((2 * HALF, (8 if n == 1 else 2) * L), BF16), stack, moved, hot(8 if n == 1 else 2), gat, pltpu.VMEM((96, Q * L), BF16),
             pltpu.VMEM(TRACE, F32), pltpu.VMEM(TRACE, F32), pltpu.VMEM((288, Q * L), BF16),
         ]
 
@@ -709,12 +792,14 @@
             args += now
         if n == 3:
             args += half_sums
-        args += [send_index]
+        args += [near_first, place] if n == 1 else [send_index]
         outs = [shape(FIELD)] * (2 * len(ending)) + [shape(TRACE)] * sum(2**c for c in ending)
         outs += [shape(TRACE)] * (3 if n == 1 else 0) + [stacked] * len(sending)
-        outs += [shape((GROUP, len(sending), MSG, 8, L))] * 2
-        scratch = common + [pltpu.VMEM((ORDER,) + FIELD, F32), msg]
+        outs += [shape((8, L), I32)] if n == 1 else []
+        outs += messages(len(sending), MSG)
+        scratch = common + [pltpu.VMEM((ORDER,) + FIELD, F32), msg(MSG)]
         scratch += [pltpu.VMEM(TRACE, F32)] * (3 if n == 3 else 0)
+        scratch += [pltpu.VMEM((2,) + FIELD, F32)] if n == 1 else []
         got = list(run(kernel, args, outs, scratch, "step%d" % n))
         for c in ending:
             fields[c] = got.pop(0)
@@ -728,7 +813,9 @@
             half_sums = [got.pop(0) for _ in range(3)]
         for c in sending:
             sources[c] = got.pop(0)
-        out_a, out_b = got
+        if n == 1:
+            send_index = got.pop(0)
+        out, cross = got
     spread = lax.all_to_all(energy_out, "dom", 0, 0, tiled=True)
     energy = jnp.sum(spread).reshape(1) / (devices * elements * Q * B)
     return final_state, energy

time: 238 us -> 202 us (0.85)
  blocking collectives: 149 us -> 72.3 us
  waiting for transfers between devices: 0 us -> 20.9 us
  starting transfers between devices: 0 us -> 17.4 us
  Pallas kernels: 74.3 us -> 76.8 us
    all_to_all x10 -> x4, blocking collectives: 131 us -> 56.6 us  [exchange(): lax.all_to_all(out, 'dom', 0, 0, axis_index_groups=aligned, tiled=True)]
    ppermute x0 -> x8, waiting for transfers between devices: none -> 20.9 us  [the longest x4 20.2 us: exchange(): got_cross = lax.ppermute(cross, 'dom', across)]
    ppermute x0 -> x8, starting transfers between devices: none -> 17.4 us  [the longest x4 15.6 us: exchange(): got_cross = lax.ppermute(cross, 'dom', across)]
    pallas_call x6 -> x5, Pallas kernels: 74.3 us -> 76.8 us  [run(): pl.pallas_call(kernel, in_specs=[smem] + [rest] * (len(args) - 1), out_sp...]
    unnamed x19 -> x24, local copies, waits for them, and re-layouts: 8.74 us -> 10.1 us
  transfers between devices with their start and end apart: 0 -> 8, of which waited for: 0 -> 5; matrix products, arithmetic and copies ran while one was open for 0% -> 0% of each run, Pallas kernels for 0% -> 0%
where the time goes in v3:
time: 202 us; the launch traced here: 201 us
  Pallas kernels  76.8 us (38%)
  blocking collectives  72.3 us (36%)
  waiting for transfers between devices  20.9 us (10%)
  starting transfers between devices  17.4 us (9%)
  local copies, waits for them, and re-layouts  10.2 us (5%)
  between operations  2.51 us (1%)
    pallas_call x5, Pallas kernels, run(): pl.pallas_call(kernel, in_specs=[smem] + [rest] * (len(args) - 1), out_sp...  76.8 us
    all_to_all x4, blocking collectives, exchange(): lax.all_to_all(out, 'dom', 0, 0, axis_index_groups=aligned, tiled=True)  56.6 us
    ppermute x4, waiting for transfers between devices, exchange(): got_cross = lax.ppermute(cross, 'dom', across)  20.2 us
    all_to_all x1, blocking collectives, shards(): spread = lax.all_to_all(energy_out, 'dom', 0, 0, tiled=True)  15.7 us
    ppermute x4, starting transfers between devices, exchange(): got_cross = lax.ppermute(cross, 'dom', across)  15.6 us
    unnamed x24, local copies, waits for them, and re-layouts  10.1 us
  transfers between devices with their start and end apart: 8, of which 5 were waited for; matrix products, arithmetic and copies ran while one was open for 0% of the time, Pallas kernels for 0%

profile of v3, /device:TPU:1, one launch (start us, length us, event | category | flops | bytes accessed | tf_op | source)
XLA Modules:
  0.0 200.8 jit_solution(2981856291394286906)
XLA Ops:
  0.7 1.1 copy-done
  1.8 1.0 copy-done.1
  2.8 1.0 copy-done.2
  3.8 1.0 copy-done.3
  4.9 0.9 copy-done.4
  10.8 22.5 %first.1 = (f32[9,56,128]{2,1,0:T(8,128)S(1)}, f32[9,56,128]{2,1,0:T(8,128)S(1)}, f32[9,56,128]{2,1,0:T(8,128)S(1)}, f32[3,81,16,128]{3,2,1,0:T(8,128)S(1)}, f32...) custom-call(s32[1]{0:T(128)} %bitcast.refs_0_, ...), custom_call_target="tpu_custom_call" | custom-call | tf_op jit(solution)/shard_map/first/pallas_call | solution.py:705
  33.3 16.0 %all_to_all.25.refs_1_ = f32[8,1,16,8,128]{4,3,2,1,0:T(8,128)S(1)} all-to-all(f32[8,1,16,8,128]{4,3,2,1,0:T(8,128)S(1)} %get-tuple-element.59), channel_id=1, replica_groups={{0,1,2,3,4,5,6,7},{8,9,10,11,12,13,14,15},{16,17,18,19,20,21,22,23},{24..., dimensions={0} | all-to-all | bytes 1048576 | tf_op jit(solution)/shard_map/all_to_all | solution.py:695
  49.3 1.4 collective-permute-start.1
  50.7 4.3 %collective-permute-start = (f32[1,1,16,8,128]{4,3,2,1,0:T(8,128)S(1)}, f32[1,1,16,8,128]{4,3,2,1,0:T(8,128)S(1)}, u32[]{:S(2)}, u32[]{:S(2)}) collective-permute-start(f32[1,1,16,8,128]{4,3,2,1,0:T(8,128)S(1)} %get-tuple-element.60), channel_id=1, source_target_pairs={{0,124},{1,125},{2,126},{3,127},{4,8},{5,9},{6,10},{7,11},{8,4},{9... | collective-permute-start | bytes 196616 | tf_op jit(solution)/shard_map/ppermute | solution.py:694
  55.0 4.5 %collective-permute-done.refs_2_ = f32[1,1,16,8,128]{4,3,2,1,0:T(8,128)S(1)} collective-permute-done((f32[1,1,16,8,128]{4,3,2,1,0:T(8,128)S(1)}, f32[1,1,16,8,128]{4,3,2,1,0:T(8,128)S(1)}, u32[]{:S(2)}, u32[]{:S(2)}) %collective-permute-start) | collective-permute-done | bytes 65568 | tf_op jit(solution)/shard_map/ppermute | solution.py:694
  59.5 12.0 %step1.1 = (f32[9,56,128]{2,1,0:T(8,128)S(1)}, f32[9,56,128]{2,1,0:T(8,128)S(1)}, f32[9,96,128]{2,1,0:T(8,128)}, f32[9,96,128]{2,1,0:T(8,128)S(1)}, f32[9,96,128...) custom-call(s32[1]{0:T(128)} %bitcast.refs_0_, ...), custom_call_target="tpu_custom_call" | custom-call | tf_op jit(solution)/shard_map/step1/pallas_call | solution.py:705
  71.6 13.8 %all_to_all.26.refs_1_ = f32[8,2,7,8,128]{4,3,2,1,0:T(8,128)S(1)} all-to-all(f32[8,2,7,8,128]{4,3,2,1,0:T(8,128)S(1)} %get-tuple-element.78), channel_id=1, replica_groups={{0,1,2,3,4,5,6,7},{8,9,10,11,12,13,14,15},{16,17,18,19,20,21,22,23},{24..., dimensions={0} | all-to-all | bytes 917504 | tf_op jit(solution)/shard_map/all_to_all | solution.py:695
  85.6 4.0 %collective-permute-start.2 = (f32[1,2,7,8,128]{4,3,2,1,0:T(8,128)S(1)}, f32[1,2,7,8,128]{4,3,2,1,0:T(8,128)S(1)}, u32[]{:S(2)}, u32[]{:S(2)}) collective-permute-start(f32[1,2,7,8,128]{4,3,2,1,0:T(8,128)S(1)} %get-tuple-element.79), channel_id=1, source_target_pairs={{0,124},{1,125},{2,126},{3,127},{4,8},{5,9},{6,10},{7,11},{8,4},{9... | collective-permute-start | bytes 172040 | tf_op jit(solution)/shard_map/ppermute | solution.py:694
  89.6 4.8 %collective-permute-done.2.refs_2_ = f32[1,2,7,8,128]{4,3,2,1,0:T(8,128)S(1)} collective-permute-done((f32[1,2,7,8,128]{4,3,2,1,0:T(8,128)S(1)}, f32[1,2,7,8,128]{4,3,2,1,0:T(8,128)S(1)}, u32[]{:S(2)}, u32[]{:S(2)}) %collective-permute-start.2) | collective-permute-done | bytes 57376 | tf_op jit(solution)/shard_map/ppermute | solution.py:694
  94.4 16.6 %step2.1 = (f32[9,56,128]{2,1,0:T(8,128)S(1)}, f32[9,56,128]{2,1,0:T(8,128)S(1)}, f32[9,56,128]{2,1,0:T(8,128)S(1)}, f32[9,56,128]{2,1,0:T(8,128)S(1)}, f32[9,96...) custom-call(s32[1]{0:T(128)} %bitcast.refs_0_, ...), custom_call_target="tpu_custom_call" | custom-call | tf_op jit(solution)/shard_map/step2/pallas_call | solution.py:705
  111.1 11.1 %all_to_all.27.refs_1_ = f32[8,1,7,8,128]{4,3,2,1,0:T(8,128)S(1)} all-to-all(f32[8,1,7,8,128]{4,3,2,1,0:T(8,128)S(1)} %get-tuple-element.88), channel_id=1, replica_groups={{0,1,2,3,4,5,6,7},{8,9,10,11,12,13,14,15},{16,17,18,19,20,21,22,23},{24..., dimensions={0} | all-to-all | bytes 458752 | tf_op jit(solution)/shard_map/all_to_all | solution.py:695
  122.3 3.6 %collective-permute-start.4 = (f32[1,1,7,8,128]{4,3,2,1,0:T(8,128)S(1)}, f32[1,1,7,8,128]{4,3,2,1,0:T(8,128)S(1)}, u32[]{:S(2)}, u32[]{:S(2)}) collective-permute-start(f32[1,1,7,8,128]{4,3,2,1,0:T(8,128)S(1)} %get-tuple-element.89), channel_id=1, source_target_pairs={{0,124},{1,125},{2,126},{3,127},{4,8},{5,9},{6,10},{7,11},{8,4},{9... | collective-permute-start | bytes 86024 | tf_op jit(solution)/shard_map/ppermute | solution.py:694
  125.9 5.1 %collective-permute-done.4.refs_2_ = f32[1,1,7,8,128]{4,3,2,1,0:T(8,128)S(1)} collective-permute-done((f32[1,1,7,8,128]{4,3,2,1,0:T(8,128)S(1)}, f32[1,1,7,8,128]{4,3,2,1,0:T(8,128)S(1)}, u32[]{:S(2)}, u32[]{:S(2)}) %collective-permute-start.4) | collective-permute-done | bytes 28704 | tf_op jit(solution)/shard_map/ppermute | solution.py:694
  131.0 12.3 %step3.1 = (f32[9,56,128]{2,1,0:T(8,128)S(1)}, f32[9,56,128]{2,1,0:T(8,128)S(1)}, f32[9,96,128]{2,1,0:T(8,128)}, bf16[448,1536]{1,0:T(8,128)(2,1)S(1)}, bf16[448...) custom-call(s32[1]{0:T(128)} %bitcast.refs_0_, ...), custom_call_target="tpu_custom_call" | custom-call | tf_op jit(solution)/shard_map/step3/pallas_call | solution.py:705
  143.3 15.8 %all_to_all.28.refs_1_ = f32[8,3,7,8,128]{4,3,2,1,0:T(8,128)S(1)} all-to-all(f32[8,3,7,8,128]{4,3,2,1,0:T(8,128)S(1)} %get-tuple-element.100), channel_id=1, replica_groups={{0,1,2,3,4,5,6,7},{8,9,10,11,12,13,14,15},{16,17,18,19,20,21,22,23},{24..., dimensions={0} | all-to-all | bytes 1376256 | tf_op jit(solution)/shard_map/all_to_all | solution.py:695
  159.2 3.6 %collective-permute-start.6 = (f32[1,3,7,8,128]{4,3,2,1,0:T(8,128)S(1)}, f32[1,3,7,8,128]{4,3,2,1,0:T(8,128)S(1)}, u32[]{:S(2)}, u32[]{:S(2)}) collective-permute-start(f32[1,3,7,8,128]{4,3,2,1,0:T(8,128)S(1)} %get-tuple-element.101), channel_id=1, source_target_pairs={{0,124},{1,125},{2,126},{3,127},{4,8},{5,9},{6,10},{7,11},{8,4},{9... | collective-permute-start | bytes 258056 | tf_op jit(solution)/shard_map/ppermute | solution.py:694
  162.8 5.8 %collective-permute-done.6.refs_2_ = f32[1,3,7,8,128]{4,3,2,1,0:T(8,128)S(1)} collective-permute-done((f32[1,3,7,8,128]{4,3,2,1,0:T(8,128)S(1)}, f32[1,3,7,8,128]{4,3,2,1,0:T(8,128)S(1)}, u32[]{:S(2)}, u32[]{:S(2)}) %collective-permute-start.6) | collective-permute-done | bytes 86048 | tf_op jit(solution)/shard_map/ppermute | solution.py:694
  169.3 13.3 %last.1 = (f32[9,56,384]{2,1,0:T(8,128)}, f32[128,1,128]{2,1,0:T(1,128)S(1)}) custom-call(s32[1]{0:T(128)} %bitcast.refs_0_, f32[8,3,7,8,128]{4,3,2,1,0:T(8,128)S(1)} %all_to_all.28.refs_1_, f32[1,3,7,8,128]{4,3,2,1,0:T(8,128)S(1)} %collective-permute-done.6.refs_2_, f32[3,3,7,8,128]{4,3,2,1,0:T(8,128)S(1)} %collective-permute-done.7.refs_3_, ...), custom_call_target="tpu_custom_call" | custom-call | tf_op jit(solution)/shard_map/last/pallas_call | solution.py:705
  182.6 15.7 %all_to_all.29 = f32[128,1,128]{2,1,0:T(1,128)S(1)} all-to-all(f32[128,1,128]{2,1,0:T(1,128)S(1)} %get-tuple-element.113), channel_id=1, replica_groups=mesh['dom'=128] {'dom'}, dimensions={0} | all-to-all | bytes 131072 | tf_op jit(solution)/shard_map/all_to_all | solution.py:819
  (31 shorter events, 6.9 us)
Async XLA Ops:
  0.7 1.1 copy-start
  1.8 1.0 copy-start.1
  2.8 1.0 copy-start.2
  3.8 1.0 copy-start.3
  4.9 0.9 copy-start.4
  5.8 0.8 copy-start.5
  6.6 0.8 copy-start.6
  7.3 0.7 copy-start.7
  8.0 0.7 copy-start.8
  8.7 0.7 copy-start.9
  9.4 0.7 copy-start.10
  10.1 0.7 copy-start.11
  49.3 10.2 %collective-permute-start.1 = (f32[3,1,16,8,128]{4,3,2,1,0:T(8,128)S(1)}, f32[3,1,16,8,128]{4,3,2,1,0:T(8,128)S(1)}, u32[]{:S(2)}, u32[]{:S(2)}) collective-permute-start(f32[3,1,16,8,128]{4,3,2,1,0:T(8,128)S(1)} %constant_dynamic-slice_fusion.3), channel_id=1, source_target_pairs={{0,8},{1,9},{2,10},{3,11},{4,124},{5,125},{6,126},{7,127},{8,16},{... | collective-permute-start | bytes 589832 | tf_op jit(solution)/shard_map/ppermute | solution.py:697
  50.7 8.8 %collective-permute-start = (f32[1,1,16,8,128]{4,3,2,1,0:T(8,128)S(1)}, f32[1,1,16,8,128]{4,3,2,1,0:T(8,128)S(1)}, u32[]{:S(2)}, u32[]{:S(2)}) collective-permute-start(f32[1,1,16,8,128]{4,3,2,1,0:T(8,128)S(1)} %get-tuple-element.60), channel_id=1, source_target_pairs={{0,124},{1,125},{2,126},{3,127},{4,8},{5,9},{6,10},{7,11},{8,4},{9... | collective-permute-start | bytes 196616 | tf_op jit(solution)/shard_map/ppermute | solution.py:694
  85.3 9.1 %collective-permute-start.3 = (f32[3,2,7,8,128]{4,3,2,1,0:T(8,128)S(1)}, f32[3,2,7,8,128]{4,3,2,1,0:T(8,128)S(1)}, u32[]{:S(2)}, u32[]{:S(2)}) collective-permute-start(f32[3,2,7,8,128]{4,3,2,1,0:T(8,128)S(1)} %constant_dynamic-slice_fusion.2), channel_id=1, source_target_pairs={{0,8},{1,9},{2,10},{3,11},{4,124},{5,125},{6,126},{7,127},{8,16},{... | collective-permute-start | bytes 516104 | tf_op jit(solution)/shard_map/ppermute | solution.py:697
  85.6 8.8 %collective-permute-start.2 = (f32[1,2,7,8,128]{4,3,2,1,0:T(8,128)S(1)}, f32[1,2,7,8,128]{4,3,2,1,0:T(8,128)S(1)}, u32[]{:S(2)}, u32[]{:S(2)}) collective-permute-start(f32[1,2,7,8,128]{4,3,2,1,0:T(8,128)S(1)} %get-tuple-element.79), channel_id=1, source_target_pairs={{0,124},{1,125},{2,126},{3,127},{4,8},{5,9},{6,10},{7,11},{8,4},{9... | collective-permute-start | bytes 172040 | tf_op jit(solution)/shard_map/ppermute | solution.py:694
  122.2 8.8 %collective-permute-start.5 = (f32[3,1,7,8,128]{4,3,2,1,0:T(8,128)S(1)}, f32[3,1,7,8,128]{4,3,2,1,0:T(8,128)S(1)}, u32[]{:S(2)}, u32[]{:S(2)}) collective-permute-start(f32[3,1,7,8,128]{4,3,2,1,0:T(8,128)S(1)} %constant_dynamic-slice_fusion.1), channel_id=1, source_target_pairs={{0,8},{1,9},{2,10},{3,11},{4,124},{5,125},{6,126},{7,127},{8,16},{... | collective-permute-start | bytes 258056 | tf_op jit(solution)/shard_map/ppermute | solution.py:697
  122.3 8.7 %collective-permute-start.4 = (f32[1,1,7,8,128]{4,3,2,1,0:T(8,128)S(1)}, f32[1,1,7,8,128]{4,3,2,1,0:T(8,128)S(1)}, u32[]{:S(2)}, u32[]{:S(2)}) collective-permute-start(f32[1,1,7,8,128]{4,3,2,1,0:T(8,128)S(1)} %get-tuple-element.89), channel_id=1, source_target_pairs={{0,124},{1,125},{2,126},{3,127},{4,8},{5,9},{6,10},{7,11},{8,4},{9... | collective-permute-start | bytes 86024 | tf_op jit(solution)/shard_map/ppermute | solution.py:694
  159.1 10.2 %collective-permute-start.7 = (f32[3,3,7,8,128]{4,3,2,1,0:T(8,128)S(1)}, f32[3,3,7,8,128]{4,3,2,1,0:T(8,128)S(1)}, u32[]{:S(2)}, u32[]{:S(2)}) collective-permute-start(f32[3,3,7,8,128]{4,3,2,1,0:T(8,128)S(1)} %constant_dynamic-slice_fusion), channel_id=1, source_target_pairs={{0,8},{1,9},{2,10},{3,11},{4,124},{5,125},{6,126},{7,127},{8,16},{... | collective-permute-start | bytes 774152 | tf_op jit(solution)/shard_map/ppermute | solution.py:697
  159.2 9.4 %collective-permute-start.6 = (f32[1,3,7,8,128]{4,3,2,1,0:T(8,128)S(1)}, f32[1,3,7,8,128]{4,3,2,1,0:T(8,128)S(1)}, u32[]{:S(2)}, u32[]{:S(2)}) collective-permute-start(f32[1,3,7,8,128]{4,3,2,1,0:T(8,128)S(1)} %get-tuple-element.101), channel_id=1, source_target_pairs={{0,124},{1,125},{2,126},{3,127},{4,8},{5,9},{6,10},{7,11},{8,4},{9... | collective-permute-start | bytes 258056 | tf_op jit(solution)/shard_map/ppermute | solution.py:694
